TPU v7x, 512 devices: a whole 4x8x8 slice. The times are simulated.
512 devices in a mesh: sec: 64 (over x, y, core), mp: 8 (over z).
Axes of the slice: x: 4, y: 8, z: 8, core: 2. Of those that a mesh axis runs over, the one named last changes fastest.
Arguments:
- inputs: bfloat16 [8192, 2048], P('sec'), may hold values from -6 to 6
- expert_w: bfloat16 [8, 2048, 1024], P('mp', 'sec'), may hold values from -0.125 to 0.125
- gate_w: bfloat16 [2048, 6, 8], replicated, may hold values from -0.125 to 0.125
- tower_up: bfloat16 [64, 1024, 4096], P('sec', None, 'mp'), as said below
- tower_out: bfloat16 [64, 4096], P('sec', 'mp'), as said below
- sections: int32 [64], replicated, may hold values from 0 to 5, as said below
- tasks: int32 [8192, 6], P('sec'), may hold values from 0 to 1, as said below
- labels: int32 [8192, 6], P('sec'), may hold values 0 or 1
Outputs:
- input_grad: bfloat16 [8192, 2048], P('sec', 'mp')
Inputs may be any that keep to these rules, and one draw needn't show every extreme that they name: `sections`: each task owns one run of consecutive indices, the runs in task order, every task at least one index. `tasks`: in each aligned block of 128 examples, task t has at most 4 times as many examples as its section has indices of sec; every task reaches this bound in some block. `tower_up`: all indices of one section hold equal copies. `tower_out`: all indices of one section hold equal copies.
All inputs are finite; a program needn't handle non-finite values. No bound on the sum of `labels` on one device may be relied on, other than what follows from the above.
Results may differ from a plain program's by a relative error of at most 0.024.
Values may be sent and summed in bfloat16 or wider, within the bound.
No kernel may reach another device: no remote copies, remote signals or barrier semaphores. Data moves between devices by JAX's collectives and lax.ppermute only.
A program may use at most 64 MiB of HBM per device.

v0:
```python
import jax
import jax.numpy as jnp
from jax import lax
from jax.sharding import PartitionSpec as P

loss_scale = 64.0


def silu_slope(value, sig):
    return sig * (1.0 + value * (1.0 - sig))


def per_device(inputs, expert_w, gate_w, tower_up, tower_out, sections, tasks, labels):
    rows = inputs.shape[0]
    task_count = tasks.shape[1]
    n_sec = lax.axis_size("sec")
    pair_slots = 2 * rows // n_sec
    slots = n_sec * pair_slots
    local_w = expert_w[0]
    width = local_w.shape[1]
    picker = (jnp.arange(gate_w.shape[2], dtype=jnp.int32) == lax.axis_index("mp")).astype(
        jnp.float32
    )
    gate_logit = jnp.einsum("nd,dtk->ntk", inputs, gate_w, preferred_element_type=jnp.float32)
    raised = jnp.exp(gate_logit)
    gates = raised / jnp.sum(raised, axis=2, keepdims=True)
    mine = jnp.sum(gates * picker, axis=2)
    whole_w = lax.all_gather(local_w, "sec", axis=0, tiled=True)
    pre = jnp.dot(inputs, whole_w, preferred_element_type=jnp.float32)
    sig_pre = jax.nn.sigmoid(pre)
    expert_out = (pre * sig_pre).astype(jnp.bfloat16)
    task_ids = jnp.arange(task_count, dtype=jnp.int32)
    members = jnp.sum((sections[None, :] == task_ids[:, None]).astype(jnp.int32), axis=1)
    first = jnp.sum((sections[None, :] < task_ids[:, None]).astype(jnp.int32), axis=1)
    ranks = jnp.cumsum(tasks, axis=0) - tasks
    target = first[None, :] + ranks % members[None, :]
    place = target * pair_slots + ranks // members[None, :]
    place = jnp.where(tasks > 0, place, slots)
    pair_total = rows * task_count
    pair_ids = jnp.arange(pair_total, dtype=jnp.int32)
    source = (
        jnp.full((slots,), pair_total, jnp.int32).at[place.reshape(-1)].set(pair_ids, mode="drop")
    )
    filled = (source < pair_total).astype(jnp.float32)
    source = jnp.minimum(source, pair_total - 1)
    src_row = source // task_count
    src_task = source % task_count
    weight = mine[src_row, src_task] * filled
    contrib = weight[:, None] * expert_out[src_row].astype(jnp.float32)
    tag_out = (filled * (1.0 + labels[src_row, src_task].astype(jnp.float32))).astype(jnp.bfloat16)
    sent = lax.psum(contrib.astype(jnp.bfloat16), "mp")
    arrived, tag_in = (
        lax.all_to_all(
            sent.reshape(n_sec, pair_slots, -1), "sec", split_axis=0, concat_axis=0, tiled=True
        ),
        lax.all_to_all(
            tag_out.reshape(n_sec, pair_slots), "sec", split_axis=0, concat_axis=0, tiled=True
        ),
    )
    arrived = arrived.reshape(slots, -1)
    up_local = tower_up[0]
    out_local = tower_out[0].astype(jnp.float32)
    act = jnp.dot(arrived, up_local, preferred_element_type=jnp.float32)
    sig_act = jax.nn.sigmoid(act)
    partial_logit = jnp.sum(act * sig_act * out_local[None, :], axis=1)
    logit = lax.psum(partial_logit, "mp")
    tag_value = tag_in.reshape(slots).astype(jnp.float32)
    alive = (tag_value > 0.5).astype(jnp.float32)
    label_value = jnp.maximum(tag_value - 1.0, 0.0)
    slope = loss_scale * (jax.nn.sigmoid(logit) - label_value) * alive
    act_grad = (slope[:, None] * out_local[None, :] * silu_slope(act, sig_act)).astype(jnp.bfloat16)
    back = lax.dot_general(
        act_grad, up_local, (((1,), (1,)), ((), ())), preferred_element_type=jnp.float32
    )
    grads = lax.psum(back.astype(jnp.bfloat16), "mp")
    returned = lax.all_to_all(
        grads.reshape(n_sec, pair_slots, -1), "sec", split_axis=0, concat_axis=0, tiled=True
    ).reshape(slots, -1)
    padded = jnp.concatenate([returned, jnp.zeros((1, width), jnp.bfloat16)], axis=0)
    mixture_grad = padded[place]
    expert_grad = jnp.zeros((rows, width), jnp.float32)
    for task in range(task_count):
        expert_grad = expert_grad + mine[:, task : task + 1] * mixture_grad[:, task].astype(
            jnp.float32
        )
    gate_grad = jnp.einsum(
        "nte,ne->nt", mixture_grad, expert_out, preferred_element_type=jnp.float32
    )
    spread_sum = lax.psum(mine * gate_grad, "mp")
    gate_logit_grad = mine * (gate_grad - spread_sum)
    pre_grad = (expert_grad * silu_slope(pre, sig_pre)).astype(jnp.bfloat16)
    gate_cols = jnp.sum(gate_w.astype(jnp.float32) * picker, axis=2)
    gate_part = jnp.dot(gate_logit_grad, gate_cols.T, precision=lax.Precision.HIGHEST)
    input_part = lax.dot_general(
        pre_grad, whole_w, (((1,), (1,)), ((), ())), preferred_element_type=jnp.float32
    )
    return lax.psum_scatter(
        (input_part + gate_part).astype(jnp.bfloat16), "mp", scatter_dimension=1, tiled=True
    )


def solution(mesh):
    in_specs = (
        P("sec", None),
        P("mp", "sec", None),
        P(),
        P("sec", None, "mp"),
        P("sec", "mp"),
        P(),
        P("sec", None),
        P("sec", None),
    )
    out_specs = P("sec", "mp")
    return jax.shard_map(
        per_device, mesh=mesh, in_specs=in_specs, out_specs=out_specs, check_vma=False
    )
```

profile of v0, /device:TPU:1, one launch (start us, length us, event | category | flops | bytes accessed | tf_op | source)
XLA Modules:
  0.0 405.0 jit_solution(17913889090033370645)
XLA Ops:
  6.5 0.7 all-gather.3.cloned.1.call-update
  7.3 0.8 copy.35
  8.1 0.7 broadcast_compare_fusion
  9.1 0.8 convert_reduce_fusion.1
  9.9 1.3 compare_select_fusion
  11.4 3.4 scatter_custom_fusion
  14.8 1.4 fusion.54
  16.3 1.4 gather_fusion.1
  17.7 1.4 gather_fusion
  19.1 81.8 %all-gather.3.cloned.1.call-done = bf16[1,2048,1024]{2,1,0:T(8,128)(2,1)} async-done(((bf16[1,32,1024]{2,1,0:T(8,128)(2,1)}), bf16[1,2048,1024]{2,1,0:T(8,128)(2,1)}) %all-gather.3.cloned.1.call-update) | async-done | bytes 4194320 | tf_op jit(solution)/shard_map/all_gather | solution.py:28
  100.8 3.8 multiply_convert_fusion.2
  104.6 1.2 gather_fusion.2
  105.9 1.0 reshape.94
  107.1 15.4 %all_to_all.20 = bf16[64,1,4]{2,1,0:T(2,128)(2,1)S(1)} all-to-all(bf16[64,1,4]{2,1,0:T(2,128)(2,1)S(1)} %all_to_all.16), channel_id=1, replica_groups=mesh['sec'=64,'mp'=8] {'sec'}, dimensions={0} | all-to-all | bytes 1024 | tf_op jit(solution)/shard_map/all_to_all | solution.py:56
  122.5 57.4 %all-reduce.4.cloned.1.call-done = bf16[64,4,1024]{2,1,0:T(4,128)(2,1)} async-done(((bf16[64,4,1024]{2,1,0:T(4,128)(2,1)}), bf16[64,4,1024]{2,1,0:T(4,128)(2,1)}) %all-reduce.4.cloned.1.call-update) | async-done | bytes 524304 | tf_op jit(solution)/shard_map/psum | solution.py:51
  179.9 14.8 %all-to-all-start.1 = ((bf16[64,4,1024]{2,1,0:T(4,128)(2,1)}), bf16[64,4,1024]{2,1,0:T(4,128)(2,1)S(1)}, u32[]{:S(2)}, u32[]{:S(2)}) async-start(bf16[64,4,1024]{2,1,0:T(4,128)(2,1)} %all-reduce.4.cloned.1.call-done), calls=%async_computation.1 | async-start | bytes 1048576 | tf_op jit(solution)/shard_map/all_to_all | solution.py:53
  195.2 16.8 %all-to-all-done.1 = bf16[64,4,1024]{2,1,0:T(4,128)(2,1)S(1)} async-done(((bf16[64,4,1024]{2,1,0:T(4,128)(2,1)}), bf16[64,4,1024]{2,1,0:T(4,128)(2,1)S(1)}, u32[]{:S(2)}, u32[]{:S(2)}) %all-to-all-start.1) | async-done | bytes 524320 | tf_op jit(solution)/shard_map/all_to_all | solution.py:53
  212.1 0.6 multiply_reduce_fusion
  212.7 12.5 %psum.29 = f32[256]{0:T(256)S(1)} all-reduce(f32[256]{0:T(256)S(1)} %get-tuple-element.29), channel_id=1, replica_groups=mesh['sec'=64,'mp'=8] {'mp'}, use_global_device_ids=true, to_apply=%region_8.9 | all-reduce | flops 256 | bytes 2048 | tf_op jit(solution)/shard_map/psum | solution.py:66
  225.2 0.6 convolution_convert_fusion
  225.9 1.0 reshape.96
  226.9 73.9 %all-reduce.6.cloned.1.call-done = bf16[64,4,1024]{2,1,0:T(4,128)(2,1)} async-done(((bf16[64,4,1024]{2,1,0:T(4,128)(2,1)}), bf16[64,4,1024]{2,1,0:T(4,128)(2,1)}) %all-reduce.6.cloned.1.call-update) | async-done | bytes 524304 | tf_op jit(solution)/shard_map/psum | solution.py:75
  300.8 14.8 %all-to-all-start.2 = ((bf16[64,4,1024]{2,1,0:T(4,128)(2,1)}), bf16[64,4,1024]{2,1,0:T(4,128)(2,1)S(1)}, u32[]{:S(2)}, u32[]{:S(2)}) async-start(bf16[64,4,1024]{2,1,0:T(4,128)(2,1)} %all-reduce.6.cloned.1.call-done), calls=%async_computation.2 | async-start | bytes 1048576 | tf_op jit(solution)/shard_map/all_to_all | solution.py:76
  316.7 16.2 %all-to-all-done.2 = bf16[64,4,1024]{2,1,0:T(4,128)(2,1)S(1)} async-done(((bf16[64,4,1024]{2,1,0:T(4,128)(2,1)}), bf16[64,4,1024]{2,1,0:T(4,128)(2,1)S(1)}, u32[]{:S(2)}, u32[]{:S(2)}) %all-to-all-start.2) | async-done | bytes 524320 | tf_op jit(solution)/shard_map/all_to_all | solution.py:76
  333.1 3.6 gather_fusion.3
  336.6 2.5 reshape.126
  339.1 3.7 fusion.53
  342.8 1.3 fusion.24
  344.2 12.5 %psum.31 = f32[128,6]{0,1:T(8,128)S(1)} all-reduce(f32[128,6]{0,1:T(8,128)S(1)} %bitcast_multiply_fusion), channel_id=1, replica_groups=mesh['sec'=64,'mp'=8] {'mp'}, use_global_device_ids=true, to_apply=%region_10.11 | all-reduce | flops 768 | bytes 6144 | tf_op jit(solution)/shard_map/psum | solution.py:89
  356.7 1.0 fusion.45
  357.8 6.1 %fusion.8 = bf16[128,2048]{1,0:T(8,128)(2,1)} fusion(f32[128,2048]{1,0:T(8,128)S(1)} %fusion.45, bf16[1,2048,1024]{2,1,0:T(8,128)(2,1)} %all-gather.3.cloned.1.call-done, f32[128,1024]{1,0:T(8,128)} %get-tuple-element.28, bf16[128,1,1024]{2,1,0:T(2,128)(2,1)} %get-tuple-element.16, bf16[128,1,1024]{2,1,0:T(2,128)(2,1)} %get-tuple-element.12, ...), kind=kOutput, calls=%fused_computation.11 | convolution fusion | flops 540803072 | bytes 7867392 | tf_op jit(solution)/shard_map/dot_general | solution.py:94
  363.9 34.6 %reduce-scatter.2.cloned.1.call-done = bf16[128,256]{1,0:T(8,128)(2,1)} async-done(((bf16[128,2048]{1,0:T(8,128)(2,1)}), bf16[128,256]{1,0:T(8,128)(2,1)}) %reduce-scatter.2.cloned.1.call-update) | async-done | bytes 65552 | tf_op jit(solution)/shard_map/reduce_scatter | solution.py:97
  (45 shorter events, 2.8 us)
Async XLA Ops:
  6.5 205.6 %copy-start = (bf16[1,1024,512]{2,1,0:T(8,128)(2,1)S(1)}, bf16[1,1024,512]{2,1,0:T(8,128)(2,1)}, u32[]{:S(2)}) copy-start(bf16[1,1024,512]{2,1,0:T(8,128)(2,1)} %param.11) | copy-start | bytes 3145732
  6.5 94.3 %copy-start.4 = (bf16[128,2048]{1,0:T(8,128)(2,1)S(1)}, bf16[128,2048]{1,0:T(8,128)(2,1)}, u32[]{:S(2)}) copy-start(bf16[128,2048]{1,0:T(8,128)(2,1)} %param.8) | copy-start | bytes 1572868
  6.5 11.1 %copy-start.1 = (s32[128,6]{0,1:T(8,128)S(1)}, s32[128,6]{0,1:T(8,128)}, u32[]{:S(2)}) copy-start(s32[128,6]{0,1:T(8,128)} %param.15) | copy-start | bytes 9220
  6.5 94.3 %all-gather.3.cloned.1.call-start = ((), (), s32[]{:S(2)}) async-start(), calls=%async_computation.7 | async-start | bytes 4259840 | tf_op jit(solution)/shard_map/all_gather | solution.py:28
  7.3 172.6 %all-reduce.4.cloned.1.call-start = ((), (), s32[]{:S(2)}) async-start(), calls=%async_computation.4 | async-start | bytes 1048576 | tf_op jit(solution)/shard_map/psum | solution.py:51
  105.8 89.0 %copy-start.3 = (bf16[1,512]{1,0:T(2,128)(2,1)S(1)}, bf16[1,512]{1,0:T(2,128)(2,1)}, u32[]{:S(2)}) copy-start(bf16[1,512]{1,0:T(2,128)(2,1)} %param.12) | copy-start | bytes 3076
  179.9 32.1 %all-to-all-start.1 = ((bf16[64,4,1024]{2,1,0:T(4,128)(2,1)}), bf16[64,4,1024]{2,1,0:T(4,128)(2,1)S(1)}, u32[]{:S(2)}, u32[]{:S(2)}) async-start(bf16[64,4,1024]{2,1,0:T(4,128)(2,1)} %all-reduce.4.cloned.1.call-done), calls=%async_computation.1 | async-start | bytes 1048576 | tf_op jit(solution)/shard_map/all_to_all | solution.py:53
  194.7 106.1 %all-reduce.6.cloned.1.call-start = ((), (), s32[]{:S(2)}) async-start(), calls=%async_computation.5 | async-start | bytes 1048576 | tf_op jit(solution)/shard_map/psum | solution.py:75
  225.8 90.1 %copy-start.2 = (bf16[2048,6,8]{0,2,1:T(8,128)(2,1)S(1)}, bf16[2048,6,8]{0,2,1:T(8,128)(2,1)}, u32[]{:S(2)}) copy-start(bf16[2048,6,8]{0,2,1:T(8,128)(2,1)} %param.10) | copy-start | bytes 589828
  300.8 32.1 %all-to-all-start.2 = ((bf16[64,4,1024]{2,1,0:T(4,128)(2,1)}), bf16[64,4,1024]{2,1,0:T(4,128)(2,1)S(1)}, u32[]{:S(2)}, u32[]{:S(2)}) async-start(bf16[64,4,1024]{2,1,0:T(4,128)(2,1)} %all-reduce.6.cloned.1.call-done), calls=%async_computation.2 | async-start | bytes 1048576 | tf_op jit(solution)/shard_map/all_to_all | solution.py:76
  315.6 82.9 %reduce-scatter.2.cloned.1.call-start = ((), (), s32[]{:S(2)}) async-start(), calls=%async_computation.6 | async-start | bytes 589824 | tf_op jit(solution)/shard_map/reduce_scatter | solution.py:97
Sparse Core Ops, SparseCore 0:
  10.7 90.0 all-gather.2
  107.1 72.7 all-reduce.3
  227.0 73.7 all-reduce.5
  364.0 34.3 reduce-scatter.1
where the time goes:
time: 410 us; the launch traced here: 405 us
  waiting for transfers between devices  281 us (69%)
  blocking collectives  40.4 us (10%)
  starting transfers between devices  29.8 us (7%)
  local copies, waits for them, and re-layouts  21.5 us (5%)
  matrix products  14.9 us (4%)
  between operations  13.4 us (3%)
    all_gather x1, waiting for transfers between devices, per_device(): whole_w = lax.all_gather(local_w, 'sec', axis=0, tiled=True)  81.8 us
    psum x1, waiting for transfers between devices, per_device(): grads = lax.psum(back.astype(jnp.bfloat16), 'mp')  73.9 us
    psum x1, waiting for transfers between devices, per_device(): sent = lax.psum(contrib.astype(jnp.bfloat16), 'mp')  57.4 us
    reduce_scatter x1, waiting for transfers between devices, per_device(): lax.psum_scatter((input_part + gate_part).astype(jnp.bfloat16), 'mp', sca...  34.6 us
    all_to_all x1, waiting for transfers between devices, per_device(): lax.all_to_all(sent.reshape(n_sec, pair_slots, -1), 'sec', split_axis=0,...  16.8 us
    all_to_all x1, waiting for transfers between devices, per_device(): lax.all_to_all(grads.reshape(n_sec, pair_slots, -1), 'sec', split_axis=0,...  16.2 us
    all_to_all x1, blocking collectives, per_device(): lax.all_to_all(tag_out.reshape(n_sec, pair_slots), 'sec', split_axis=0, c...  15.4 us
    all_to_all x1, starting transfers between devices, per_device(): lax.all_to_all(sent.reshape(n_sec, pair_slots, -1), 'sec', split_axis=0,...  14.8 us
  transfers between devices with their start and end apart: 6, of which 6 were waited for; matrix products, arithmetic and copies ran while one was open for 3% of the time, Pallas kernels for 0%

commit v1 on v0

v1 whole, which is shorter than its diff:
```python
import jax
import jax.numpy as jnp
from jax import lax
from jax.sharding import Mesh, PartitionSpec as P

loss_scale = 64.0
NX, NY, NC = 4, 8, 2


def silu_slope(value, sig):
    return sig * (1.0 + value * (1.0 - sig))


def split_two(value):
    high = lax.reduce_precision(value, 8, 7)
    return high.astype(jnp.bfloat16), (value - high).astype(jnp.bfloat16)


def per_device(inputs, expert_w, gate_w, tower_up, tower_out, sections, tasks, labels):
    f32, bf16 = jnp.float32, jnp.bfloat16
    rows, din = inputs.shape
    tn = tasks.shape[1]
    n_mp = lax.axis_size("mp")
    n_sec = NX * NY * NC
    kn = gate_w.shape[2]
    part_d, width = expert_w.shape[1:]
    cols = width // n_mp
    pair_slots = 2 * rows // n_sec
    slots = n_sec * pair_slots
    sec_axes = ("x", "y", "c")

    block = expert_w[0].reshape(part_d, n_mp, cols).transpose(1, 0, 2)
    block = jnp.broadcast_to(block[None], (NY, n_mp, part_d, cols))
    part = lax.all_to_all(
        block.reshape(NY * n_mp, part_d, cols), ("y", "mp"), 0, 0, tiled=True
    )
    wide = lax.all_to_all(
        jnp.broadcast_to(part[None], (NX,) + part.shape), "x", 0, 0, tiled=True
    )
    other = lax.ppermute(wide, "c", [(0, 1), (1, 0)])
    core = lax.axis_index("c")
    zero = jnp.where(core == 0, wide, other).reshape(NX * NY, 1, kn, part_d, cols)
    one = jnp.where(core == 0, other, wide).reshape(NX * NY, 1, kn, part_d, cols)
    whole = jnp.concatenate([zero, one], axis=1).reshape(n_sec, kn, part_d, cols)
    w_all = whole.transpose(0, 2, 1, 3).reshape(din, kn * cols)

    gate_logit = jnp.einsum("nd,dtk->ntk", inputs, gate_w, preferred_element_type=f32)
    raised = jnp.exp(gate_logit)
    gates = raised / jnp.sum(raised, axis=2, keepdims=True)
    task_ids = jnp.arange(tn, dtype=jnp.int32)
    members = jnp.sum((sections[None, :] == task_ids[:, None]).astype(jnp.int32), axis=1)
    first = jnp.sum((sections[None, :] < task_ids[:, None]).astype(jnp.int32), axis=1)
    ranks = jnp.cumsum(tasks, axis=0) - tasks
    turn = jnp.zeros_like(ranks)
    for step in range(1, pair_slots):
        turn = turn + (ranks >= step * members[None, :]).astype(jnp.int32)
    place = (first[None, :] + ranks - turn * members[None, :]) * pair_slots + turn
    place = jnp.where(tasks > 0, place, slots).reshape(1, rows * tn)
    pick = (place == jnp.arange(slots, dtype=jnp.int32)[:, None]).astype(bf16)

    pre = jnp.dot(inputs, w_all, preferred_element_type=f32).reshape(rows, kn, cols)
    sig_pre = jax.nn.sigmoid(pre)
    expert_out = (pre * sig_pre).astype(bf16)
    wide_out = expert_out.astype(f32)
    mixture = gates[:, :, 0, None] * wide_out[:, None, 0]
    for k in range(1, kn):
        mixture = mixture + gates[:, :, k, None] * wide_out[:, None, k]
    mixture = mixture.astype(bf16).reshape(rows * tn, cols)
    sent = jnp.dot(pick, mixture, preferred_element_type=f32).astype(bf16)
    sent = jnp.broadcast_to(
        sent.reshape(1, n_sec, pair_slots, cols), (n_mp, n_sec, pair_slots, cols)
    ).reshape(n_mp * n_sec, pair_slots, cols)
    arrived = lax.all_to_all(sent, ("mp",) + sec_axes, 0, 0, tiled=True)

    up = tower_up[0]
    out_w = tower_out[0].astype(f32)
    rows_in = arrived.reshape(n_mp, slots, cols).transpose(1, 0, 2).reshape(slots, width)
    act = jnp.dot(rows_in, up, preferred_element_type=f32)
    sig_act = jax.nn.sigmoid(act)
    logit_part = jnp.sum(act * sig_act * out_w[None, :], axis=1)
    act_grad = (out_w[None, :] * silu_slope(act, sig_act)).astype(bf16)
    back = lax.dot_general(
        act_grad, up, (((1,), (1,)), ((), ())), preferred_element_type=f32
    ).astype(bf16)
    back = back.reshape(slots, n_mp, cols).transpose(1, 0, 2)
    high, low = split_two(logit_part)
    extra = jnp.concatenate([high.reshape(-1, cols), low.reshape(-1, cols)], axis=0)
    n_extra = extra.shape[0]
    extra = jnp.concatenate([extra, jnp.zeros((16 - n_extra, cols), bf16)], axis=0)
    extra = jnp.broadcast_to(extra[None], (n_mp, 16, cols))
    summed = lax.all_to_all(jnp.concatenate([back, extra], axis=1), "mp", 0, 0, tiled=True)
    total = jnp.sum(summed.astype(f32), axis=0)
    logit = (total[slots : slots + n_extra // 2] + total[slots + n_extra // 2 : slots + n_extra])
    high, low = split_two(logit.reshape(n_sec, pair_slots))
    tail = jnp.concatenate([high, low], axis=1)
    tail = jnp.pad(tail, ((0, 0), (0, cols - 2 * pair_slots)))[:, None]
    body = total[:slots].astype(bf16).reshape(n_sec, pair_slots, cols)
    fill = jnp.zeros((n_sec, 8 - pair_slots - 1, cols), bf16)
    home = lax.all_to_all(
        jnp.concatenate([body, tail, fill], axis=1), sec_axes, 0, 0, tiled=True
    )
    grads = home[:, :pair_slots].reshape(slots, cols)
    logits = home[:, pair_slots, : 2 * pair_slots].reshape(n_sec, 2, pair_slots)
    logits = logits.transpose(0, 2, 1).reshape(slots, 2)

    stacked = jnp.concatenate([grads, logits, jnp.zeros((slots, cols - 2), bf16)], axis=1)
    rows_back = lax.dot_general(
        pick, stacked, (((0,), (0,)), ((), ())), preferred_element_type=f32
    ).reshape(rows, tn, 2 * cols)
    logit_home = rows_back[:, :, cols] + rows_back[:, :, cols + 1]
    slope = loss_scale * (jax.nn.sigmoid(logit_home) - labels.astype(f32)) * tasks.astype(f32)
    mixture_grad = (slope[:, :, None] * rows_back[:, :, :cols]).astype(bf16).astype(f32)
    expert_grad = gates[:, 0, :, None] * mixture_grad[:, 0, None]
    for task in range(1, tn):
        expert_grad = expert_grad + gates[:, task, :, None] * mixture_grad[:, task, None]
    gate_grad = jnp.sum(mixture_grad[:, :, None, :] * wide_out[:, None, :, :], axis=3)
    spread = jnp.sum(gates * gate_grad, axis=2, keepdims=True)
    gate_logit_grad = gates * (gate_grad - spread)
    pre_grad = (expert_grad * silu_slope(pre, sig_pre)).astype(bf16).reshape(rows, kn * cols)
    gate_part = jnp.dot(
        gate_logit_grad.reshape(rows, tn * kn),
        gate_w.astype(f32).reshape(din, tn * kn).T,
        precision=lax.Precision.HIGHEST,
    )
    input_part = lax.dot_general(
        pre_grad, w_all, (((1,), (1,)), ((), ())), preferred_element_type=f32
    )
    partial = (input_part + gate_part).astype(bf16)
    partial = partial.reshape(rows, n_mp, din // n_mp).transpose(1, 0, 2)
    pieces = lax.all_to_all(partial, "mp", 0, 0, tiled=True)
    return jnp.sum(pieces.astype(f32), axis=0).astype(bf16)


def solution(mesh):
    grid = Mesh(
        mesh.devices.reshape(NX, NY, NC, mesh.shape["mp"]), ("x", "y", "c", "mp")
    )
    sec = ("x", "y", "c")
    in_specs = (
        P(sec, None),
        P("mp", sec, None),
        P(),
        P(sec, None, "mp"),
        P(sec, "mp"),
        P(),
        P(sec, None),
        P(sec, None),
    )
    return jax.shard_map(
        per_device, mesh=grid, in_specs=in_specs, out_specs=P(sec, "mp"), check_vma=False
    )
```

time: 410 us -> 205 us (0.50); the launches traced: 405 us -> 205 us
  waiting for transfers between devices: 281 us -> 51.3 us
  blocking collectives: 40.4 us -> 80.1 us
  between operations: 13.4 us -> 0.68 us
  local copies, waits for them, and re-layouts: 21.5 us -> 29.1 us
  starting transfers between devices: 29.8 us -> 25 us
    psum x2 -> x0, waiting for transfers between devices: 131 us -> none  [the longest x1 73.9 us: per_device(): grads = lax.psum(back.astype(jnp.bfloat16), 'mp')]
    all_gather x1 -> x0, waiting for transfers between devices: 81.8 us -> none  [per_device(): whole_w = lax.all_gather(local_w, 'sec', axis=0, tiled=True)]
    all_to_all x1 -> x3, blocking collectives: 15.4 us -> 80.1 us  [the longest x1 33.4 us: per_device(): lax.all_to_all(block.reshape(NY * n_mp, part_d, cols), ('y', 'mp'), 0, 0,...]
    reduce_scatter x1 -> x0, waiting for transfers between devices: 34.6 us -> none  [per_device(): lax.psum_scatter((input_part + gate_part).astype(jnp.bfloat16), 'mp', sca...]
    psum x2 -> x0, blocking collectives: 25 us -> none  [the longest x1 12.5 us: per_device(): spread_sum = lax.psum(mine * gate_grad, 'mp')]
    all_to_all x2 -> x3, waiting for transfers between devices: 32.9 us -> 51.3 us  [the longest x1 22.6 us: per_device(): arrived = lax.all_to_all(sent, ('mp',) + sec_axes, 0, 0, tiled=True)]
    mul x1 -> x41, local copies, waits for them, and re-layouts: 0.54 us -> 15.4 us  [the longest x28 13.8 us: per_device(): mixture = mixture + gates[:, :, k, None] * wide_out[:, None, k]]
    all_to_all x2 -> x3, starting transfers between devices: 29.5 us -> 18.4 us  [the longest x1 10.3 us: per_device(): arrived = lax.all_to_all(sent, ('mp',) + sec_axes, 0, 0, tiled=True)]
  transfers between devices with their start and end apart: 6 -> 4, of which waited for: 6 -> 3; matrix products, arithmetic and copies ran while one was open for 3% -> 3% of each run, Pallas kernels for 0% -> 0%
where the time goes in v1:
time: 205 us
  blocking collectives  80.1 us (39%)
  waiting for transfers between devices  51.3 us (25%)
  local copies, waits for them, and re-layouts  29.1 us (14%)
  starting transfers between devices  25 us (12%)
  matrix products  11.5 us (6%)
  other arithmetic  6.9 us (3%)
    all_to_all x1, blocking collectives, per_device(): lax.all_to_all(block.reshape(NY * n_mp, part_d, cols), ('y', 'mp'), 0, 0,...  33.4 us
    all_to_all x1, blocking collectives, per_device(): lax.all_to_all(jnp.broadcast_to(part[None], (NX,) + part.shape), 'x', 0,...  26.4 us
    all_to_all x1, waiting for transfers between devices, per_device(): arrived = lax.all_to_all(sent, ('mp',) + sec_axes, 0, 0, tiled=True)  22.6 us
    all_to_all x1, blocking collectives, per_device(): pieces = lax.all_to_all(partial, 'mp', 0, 0, tiled=True)  20.3 us
    all_to_all x1, waiting for transfers between devices, per_device(): lax.all_to_all(jnp.concatenate([back, extra], axis=1), 'mp', 0, 0, tiled=...  18.6 us
    mul x28, local copies, waits for them, and re-layouts, per_device(): mixture = mixture + gates[:, :, k, None] * wide_out[:, None, k]  13.8 us
    all_to_all x1, starting transfers between devices, per_device(): arrived = lax.all_to_all(sent, ('mp',) + sec_axes, 0, 0, tiled=True)  10.3 us
    all_to_all x1, waiting for transfers between devices, per_device(): lax.all_to_all(jnp.concatenate([body, tail, fill], axis=1), sec_axes, 0,...  10.1 us
  transfers between devices with their start and end apart: 4, of which 3 were waited for; matrix products, arithmetic and copies ran while one was open for 3% of the time, Pallas kernels for 0%

profile of v1, /device:TPU:1, one launch (start us, length us, event | category | flops | bytes accessed | tf_op | source)
XLA Modules:
  0.0 204.6 jit_solution(549103466488753156)
XLA Ops:
  0.0 0.9 copy.272
  1.1 33.4 %all_to_all.30 = bf16[64,32,128]{2,1,0:T(8,128)(2,1)S(1)} all-to-all(bf16[64,32,128]{2,1,0:T(8,128)(2,1)S(1)} %bitcast.166), channel_id=1, replica_groups=mesh['x'=4,'y'=8,'c'=2,'mp'=8] {'y','mp'}, dimensions={0} | all-to-all | bytes 1048576 | tf_op jit(solution)/shard_map/all_to_all | solution.py:34
  34.8 26.4 %all_to_all.31 = bf16[4,64,32,128]{3,2,1,0:T(8,128)(2,1)S(1)} all-to-all(bf16[4,64,32,128]{3,2,1,0:T(8,128)(2,1)S(1)} %broadcast_in_dim.24), channel_id=1, replica_groups=mesh['x'=4,'y'=8,'c'=2,'mp'=8] {'x'}, dimensions={0} | all-to-all | bytes 4194304 | tf_op jit(solution)/shard_map/all_to_all | solution.py:37
  61.2 6.6 %collective-permute-start = (bf16[4,64,32,128]{3,2,1,0:T(8,128)(2,1)S(1)}, bf16[4,64,32,128]{3,2,1,0:T(8,128)(2,1)}, u32[]{:S(2)}, u32[]{:S(2)}) collective-permute-start(bf16[4,64,32,128]{3,2,1,0:T(8,128)(2,1)S(1)} %all_to_all.31), channel_id=1, source_target_pairs={{0,8},{8,0},{1,9},{9,1},{2,10},{10,2},{3,11},{11,3},{4,12},{12,4},... | collective-permute-start | bytes 6291464 | tf_op jit(solution)/shard_map/ppermute | solution.py:40
  67.8 1.4 fusion.49
  73.9 1.9 broadcast_select_fusion.1
  76.2 4.2 %copy.225 = bf16[64,32,8,128]{3,2,1,0:T(8,128)(2,1)S(1)} copy(bf16[64,32,8,128]{3,1,2,0:T(8,128)(2,1)S(1)} %bitcast.157) | data formatting | bytes 8388608 | tf_op jit(solution)/shard_map/transpose | solution.py:45
  80.4 1.3 fusion.2
  82.3 0.8 copy-done.2
  84.5 1.6 copy.232
  86.1 0.9 mul.421
  86.9 0.8 mul.422
  87.8 1.6 copy.234
  89.3 0.9 mul.427
  91.7 0.9 mul.433
  92.6 0.8 mul.434
  93.5 0.8 mul.440
  94.5 0.8 mul.446
  95.3 2.9 %convolution_convert_fusion.1 = bf16[256,128]{1,0:T(8,128)(2,1)S(1)} fusion(s32[768]{0:T(1024)S(1)} %eq.13, f32[768,128]{1,0:T(8,128)} %mul.446, f32[768,128]{1,0:T(8,128)} %mul.440, f32[768,128]{1,0:T(8,128)} %mul.434, f32[768,128]{1,0:T(8,128)} %mul.428, f32[768,128]{1,0:T(8,128)} %mul.422, f32[768,128]{1,0:T(8,128)S(1)} %mul.416, ...), kind=kOutput, calls=%fused_computation.15 | convolution fusion | flops 52133888 | bytes 3238912 | tf_op jit(solution)/shard_map/dot_general | solution.py:69
  98.2 1.0 broadcast_in_dim.26
  99.1 10.3 %all-to-all-start.2 = ((bf16[512,4,128]{2,1,0:T(4,128)(2,1)}), bf16[512,4,128]{2,1,0:T(4,128)(2,1)S(1)}, u32[]{:S(2)}, u32[]{:S(2)}) async-start(bf16[512,4,128]{2,1,0:T(4,128)(2,1)} %bitcast.22), calls=%async_computation.2 | async-start | bytes 1048576 | tf_op jit(solution)/shard_map/all_to_all | solution.py:73
  109.6 22.6 %all-to-all-done.2 = bf16[512,4,128]{2,1,0:T(4,128)(2,1)S(1)} async-done(((bf16[512,4,128]{2,1,0:T(4,128)(2,1)}), bf16[512,4,128]{2,1,0:T(4,128)(2,1)S(1)}, u32[]{:S(2)}, u32[]{:S(2)}) %all-to-all-start.2) | async-done | bytes 524320 | tf_op jit(solution)/shard_map/all_to_all | solution.py:73
  133.8 0.9 pad_maximum_fusion.1
  134.6 3.5 %all-to-all-start.3 = ((bf16[8,272,128]{2,1,0:T(8,128)(2,1)}), bf16[8,272,128]{2,1,0:T(8,128)(2,1)S(1)}, u32[]{:S(2)}, u32[]{:S(2)}) async-start(bf16[8,272,128]{2,1,0:T(8,128)(2,1)} %pad_maximum_fusion.1), calls=%async_computation.3 | async-start | bytes 1114112 | tf_op jit(solution)/shard_map/all_to_all | solution.py:91
  138.3 18.6 %all-to-all-done.3 = bf16[8,272,128]{2,1,0:T(8,128)(2,1)S(1)} async-done(((bf16[8,272,128]{2,1,0:T(8,128)(2,1)}), bf16[8,272,128]{2,1,0:T(8,128)(2,1)S(1)}, u32[]{:S(2)}, u32[]{:S(2)}) %all-to-all-start.3) | async-done | bytes 557088 | tf_op jit(solution)/shard_map/all_to_all | solution.py:91
  158.0 4.5 %all-to-all-start.4 = ((bf16[64,8,128]{2,1,0:T(8,128)(2,1)}), bf16[64,8,128]{2,1,0:T(8,128)(2,1)S(1)}, u32[]{:S(2)}, u32[]{:S(2)}) async-start(bf16[64,8,128]{2,1,0:T(8,128)(2,1)} %maximum_maximum_fusion), calls=%async_computation.4 | async-start | bytes 262144 | tf_op jit(solution)/shard_map/all_to_all | solution.py:99
  162.8 10.1 %all-to-all-done.4 = bf16[64,8,128]{2,1,0:T(8,128)(2,1)S(1)} async-done(((bf16[64,8,128]{2,1,0:T(8,128)(2,1)}), bf16[64,8,128]{2,1,0:T(8,128)(2,1)S(1)}, u32[]{:S(2)}, u32[]{:S(2)}) %all-to-all-start.4) | async-done | bytes 131104 | tf_op jit(solution)/shard_map/all_to_all | solution.py:99
  173.8 1.0 fusion.46
  175.0 1.3 copy.269
  176.9 0.9 multiply_reduce_fusion
  179.1 3.7 %fusion = f32[128,2048]{1,0:T(8,128)S(1)} fusion(bf16[128,1024]{0,1:T(8,128)(2,1)S(1)} %fusion.15, bf16[256,8,8,128]{3,2,1,0:T(8,128)(2,1)} %bitcast.161), kind=kOutput, calls=%fused_computation | convolution fusion | flops 536870912 | bytes 5505024 | tf_op jit(solution)/shard_map/dot_general | solution.py:125
  183.5 20.3 %all_to_all.32 = bf16[8,128,256]{2,1,0:T(8,128)(2,1)S(1)} all-to-all(bf16[8,128,256]{2,1,0:T(8,128)(2,1)S(1)} %bitcast.167), channel_id=1, replica_groups=mesh['x'=4,'y'=8,'c'=2,'mp'=8] {'mp'}, dimensions={0} | all-to-all | bytes 1048576 | tf_op jit(solution)/shard_map/all_to_all | solution.py:130
  (119 shorter events, 16.5 us)
Async XLA Ops:
  0.0 132.4 %copy-start = (bf16[1,1024,512]{2,1,0:T(8,128)(2,1)S(1)}, bf16[1,1024,512]{2,1,0:T(8,128)(2,1)}, u32[]{:S(2)}) copy-start(bf16[1,1024,512]{2,1,0:T(8,128)(2,1)} %param.11) | copy-start | bytes 3145732
  34.4 33.4 %copy-start.4 = (bf16[2048,6,8]{0,2,1:T(8,128)(2,1)S(1)}, bf16[2048,6,8]{0,2,1:T(8,128)(2,1)}, u32[]{:S(2)}) copy-start(bf16[2048,6,8]{0,2,1:T(8,128)(2,1)} %param.10) | copy-start | bytes 589828
  34.8 38.2 %copy-start.7 = (s32[128,6]{0,1:T(8,128)S(1)}, s32[128,6]{0,1:T(8,128)}, u32[]{:S(2)}) copy-start(s32[128,6]{0,1:T(8,128)} %param.14) | copy-start | bytes 9220
  34.8 38.6 %copy-start.10 = (s32[64]{0:T(128)S(1)}, s32[64]{0:T(128)}, u32[]{:S(2)}) copy-start(s32[64]{0:T(128)} %param.13) | copy-start | bytes 772
  61.2 12.7 %collective-permute-start = (bf16[4,64,32,128]{3,2,1,0:T(8,128)(2,1)S(1)}, bf16[4,64,32,128]{3,2,1,0:T(8,128)(2,1)}, u32[]{:S(2)}, u32[]{:S(2)}) collective-permute-start(bf16[4,64,32,128]{3,2,1,0:T(8,128)(2,1)S(1)} %all_to_all.31), channel_id=1, source_target_pairs={{0,8},{8,0},{1,9},{9,1},{2,10},{10,2},{3,11},{11,3},{4,12},{12,4},... | collective-permute-start | bytes 6291464 | tf_op jit(solution)/shard_map/ppermute | solution.py:40
  76.2 4.2 %copy-start.6 = (bf16[128,2048]{1,0:T(8,128)(2,1)S(1)}, bf16[128,2048]{1,0:T(8,128)(2,1)}, u32[]{:S(2)}) copy-start(bf16[128,2048]{1,0:T(8,128)(2,1)} %param.8) | copy-start | bytes 1572868
  80.3 1.9 copy-start.1
  82.3 0.8 copy-start.2
  94.5 15.0 %copy-start.9 = (bf16[1,512]{1,0:T(2,128)(2,1)S(1)}, bf16[1,512]{1,0:T(2,128)(2,1)}, u32[]{:S(2)}) copy-start(bf16[1,512]{1,0:T(2,128)(2,1)} %param.12) | copy-start | bytes 3076
  99.1 33.1 %all-to-all-start.2 = ((bf16[512,4,128]{2,1,0:T(4,128)(2,1)}), bf16[512,4,128]{2,1,0:T(4,128)(2,1)S(1)}, u32[]{:S(2)}, u32[]{:S(2)}) async-start(bf16[512,4,128]{2,1,0:T(4,128)(2,1)} %bitcast.22), calls=%async_computation.2 | async-start | bytes 1048576 | tf_op jit(solution)/shard_map/all_to_all | solution.py:73
  134.6 22.2 %all-to-all-start.3 = ((bf16[8,272,128]{2,1,0:T(8,128)(2,1)}), bf16[8,272,128]{2,1,0:T(8,128)(2,1)S(1)}, u32[]{:S(2)}, u32[]{:S(2)}) async-start(bf16[8,272,128]{2,1,0:T(8,128)(2,1)} %pad_maximum_fusion.1), calls=%async_computation.3 | async-start | bytes 1114112 | tf_op jit(solution)/shard_map/all_to_all | solution.py:91
  158.0 15.0 %all-to-all-start.4 = ((bf16[64,8,128]{2,1,0:T(8,128)(2,1)}), bf16[64,8,128]{2,1,0:T(8,128)(2,1)S(1)}, u32[]{:S(2)}, u32[]{:S(2)}) async-start(bf16[64,8,128]{2,1,0:T(8,128)(2,1)} %maximum_maximum_fusion), calls=%async_computation.4 | async-start | bytes 262144 | tf_op jit(solution)/shard_map/all_to_all | solution.py:99
  162.8 13.5 %copy-start.8 = (s32[128,6]{0,1:T(8,128)S(1)}, s32[128,6]{0,1:T(8,128)}, u32[]{:S(2)}) copy-start(s32[128,6]{0,1:T(8,128)} %param.15) | copy-start | bytes 9220
  175.0 3.8 %copy-start.3 = (f32[1024,128]{1,0:T(8,128)S(1)}, f32[1024,128]{1,0:T(8,128)}, u32[]{:S(2)}) copy-start(f32[1024,128]{1,0:T(8,128)} %copy-done.2) | copy-start | bytes 1572868
  179.0 3.8 %copy-start.5 = (bf16[2048,6,8]{0,2,1:T(8,128)(2,1)S(1)}, bf16[2048,6,8]{0,2,1:T(8,128)(2,1)}, u32[]{:S(2)}) copy-start(bf16[2048,6,8]{0,2,1:T(8,128)(2,1)} %param.10) | copy-start | bytes 589828

commit v2 on v1

v2 whole, which is shorter than its diff:
```python
import jax
import jax.numpy as jnp
from jax import lax
from jax.experimental import pallas as pl
from jax.experimental.pallas import tpu as pltpu
from jax.sharding import Mesh, PartitionSpec as P

loss_scale = 64.0
NX, NY, NC = 4, 8, 2


def silu_slope(value, sig):
    return sig * (1.0 + value * (1.0 - sig))


def split_two(value):
    high = lax.reduce_precision(value, 8, 7)
    return high.astype(jnp.bfloat16), (value - high).astype(jnp.bfloat16)


def group_sum(value, group):
    n = value.shape[1]
    row = lax.broadcasted_iota(jnp.int32, (n, n), 0) // group
    col = lax.broadcasted_iota(jnp.int32, (n, n), 1) // group
    ones = (row == col).astype(jnp.float32)
    return jnp.dot(
        value, ones, precision=lax.Precision.HIGHEST, preferred_element_type=jnp.float32
    )


def gate_kernel(tn, kn, pair_slots):
    f32, bf16 = jnp.float32, jnp.bfloat16

    def kernel(x_ref, gw_ref, sec_ref, task_ref, gate_ref, row_ref, col_ref):
        logit = jnp.dot(x_ref[...], gw_ref[...], preferred_element_type=f32)
        raised = jnp.exp(logit)
        gate_ref[...] = raised / group_sum(raised, kn)

        n_sec = sec_ref.shape[1]
        rows = task_ref.shape[0]
        sec_row = sec_ref[...]
        task = task_ref[...].astype(f32)
        task16 = task.astype(bf16)
        one = lax.broadcasted_iota(jnp.int32, (rows, rows), 0)
        two = lax.broadcasted_iota(jnp.int32, (rows, rows), 1)
        below = (two < one).astype(f32).astype(bf16)
        above = (one < two).astype(f32).astype(bf16)
        same = (one == two).astype(f32).astype(bf16)
        across = (((0,), (0,)), ((), ()))
        rank_col = jnp.dot(below, task16, preferred_element_type=f32)
        rank_row = lax.dot_general(task16, above, across, preferred_element_type=f32)
        task_row = lax.dot_general(task16, same, across, preferred_element_type=f32)

        ids_row = lax.broadcasted_iota(jnp.int32, (tn, n_sec), 0)
        hit = (sec_row == ids_row).astype(f32)
        less = (sec_row < ids_row).astype(f32)
        member_col = jnp.sum(hit, axis=1, keepdims=True)
        first_col = jnp.sum(less, axis=1, keepdims=True)
        eye = lax.broadcasted_iota(jnp.int32, (tn, tn), 0) == lax.broadcasted_iota(
            jnp.int32, (tn, tn), 1
        )
        member_row = jnp.sum(jnp.where(eye, member_col, 0.0), axis=0, keepdims=True)
        first_row = jnp.sum(jnp.where(eye, first_col, 0.0), axis=0, keepdims=True)

        def find(rank, member, first, active):
            turn = jnp.zeros_like(rank)
            for step in range(1, pair_slots):
                turn = turn + (rank >= step * member).astype(f32)
            target = first + rank - turn * member
            return jnp.where(active > 0.5, target, -1000.0), turn

        target, turn = find(rank_row, member_col, first_col, task_row)
        row_ref[0:tn, :] = target
        row_ref[tn : 2 * tn, :] = turn
        target, turn = find(rank_col, member_row, first_row, task)
        col_ref[:, 0:tn] = target
        col_ref[:, tn : 2 * tn] = turn

    return kernel


def load_weights(core_ref, own_ref, other_ref, w_ref, sems):
    def run(own_at, finish):
        first = pltpu.make_async_copy(own_ref, w_ref.at[:, own_at], sems.at[0])
        second = pltpu.make_async_copy(other_ref, w_ref.at[:, 1 - own_at], sems.at[1])
        if finish:
            first.wait()
            second.wait()
        else:
            first.start()
            second.start()

    def both(finish):
        @pl.when(core_ref[0] == 0)
        def _():
            run(0, finish)

        @pl.when(core_ref[0] != 0)
        def _():
            run(1, finish)

    return lambda: both(False), lambda: both(True)


def pair_weights(w_ref, k, lo, hi):
    part_d, cols = w_ref.shape[3:]
    count = (hi - lo) * w_ref.shape[1] * part_d
    return jnp.concatenate(
        [w_ref[lo:hi, :, k + i].reshape(count, cols) for i in range(2)], axis=1
    )


def forward_kernel(tn, kn, pair_slots, n_mp):
    f32, bf16 = jnp.float32, jnp.bfloat16

    def kernel(core_ref, own_ref, other_ref, x_ref, gate_ref, row_ref, sent_ref, pre_ref, w_ref, sems):
        start, wait = load_weights(core_ref, own_ref, other_ref, w_ref, sems)
        start()
        rows = x_ref.shape[0]
        slots, cols = sent_ref.shape[1:]
        slot_id = lax.broadcasted_iota(jnp.int32, (slots, rows), 0).astype(f32)
        picks = []
        for t in range(tn):
            place = row_ref[t : t + 1, :] * pair_slots + row_ref[tn + t : tn + t + 1, :]
            picks.append((slot_id == place).astype(f32).astype(bf16))
        pick = jnp.concatenate(picks, axis=1)
        wait()
        x = x_ref[...]
        mix = [jnp.zeros((rows, cols), f32) for _ in range(tn)]
        for k in range(0, kn, 2):
            pre = jnp.dot(
                x, pair_weights(w_ref, k, 0, w_ref.shape[0]), preferred_element_type=f32
            )
            pre_ref[:, k * cols : (k + 2) * cols] = pre
            out = (pre * jax.nn.sigmoid(pre)).astype(bf16).astype(f32)
            for i in range(2):
                part = out[:, i * cols : (i + 1) * cols]
                for t in range(tn):
                    at = t * kn + k + i
                    mix[t] = mix[t] + gate_ref[:, at : at + 1] * part
        stack = jnp.concatenate([m.astype(bf16) for m in mix], axis=0)
        sent = jnp.dot(pick, stack, preferred_element_type=f32).astype(bf16)
        for m in range(n_mp):
            sent_ref[m] = sent

    return kernel


def backward_kernel(tn, kn, pair_slots, n_mp):
    f32, bf16 = jnp.float32, jnp.bfloat16

    def kernel(
        core_ref, own_ref, other_ref, home_ref, gate_ref, col_ref, pre_ref,
        label_ref, task_ref, gw_ref, out_ref, w_ref, sems,
    ):
        start, wait = load_weights(core_ref, own_ref, other_ref, w_ref, sems)
        start()
        total, cols = home_ref.shape
        rows = gate_ref.shape[0]
        home = home_ref[...]
        lane = lax.broadcasted_iota(jnp.int32, (rows, total), 1).astype(f32)
        lane_c = lax.broadcasted_iota(jnp.int32, (rows, cols), 1).astype(f32)
        grads = []
        for t in range(tn):
            target = col_ref[:, t : t + 1] * 8.0
            turn = col_ref[:, tn + t : tn + t + 1]
            pick = (lane == target + turn).astype(f32).astype(bf16)
            pick_tail = (lane == target + pair_slots).astype(f32).astype(bf16)
            got = jnp.dot(pick, home, preferred_element_type=f32)
            tail = jnp.dot(pick_tail, home, preferred_element_type=f32)
            chosen = (lane_c == turn) | (lane_c == turn + pair_slots)
            logit = jnp.sum(jnp.where(chosen, tail, 0.0), axis=1, keepdims=True)
            label = label_ref[:, t : t + 1].astype(f32)
            alive = task_ref[:, t : t + 1].astype(f32)
            slope = loss_scale * (jax.nn.sigmoid(logit) - label) * alive
            grads.append((slope * got).astype(bf16).astype(f32))
        gates = gate_ref[...]
        gate_grad = jnp.zeros((rows, tn * kn), f32)
        lane_g = lax.broadcasted_iota(jnp.int32, (rows, tn * kn), 1)
        pre_grads = []
        for k in range(kn):
            pre = pre_ref[:, k * cols : (k + 1) * cols]
            sig = jax.nn.sigmoid(pre)
            out = (pre * sig).astype(bf16).astype(f32)
            grad = jnp.zeros((rows, cols), f32)
            for t in range(tn):
                at = t * kn + k
                grad = grad + gate_ref[:, at : at + 1] * grads[t]
                dot = jnp.sum(grads[t] * out, axis=1, keepdims=True)
                gate_grad = jnp.where(lane_g == at, dot, gate_grad)
            pre_grads.append((grad * silu_slope(pre, sig)).astype(bf16))
        spread = group_sum(gates * gate_grad, kn)
        logit_grad = gates * (gate_grad - spread)
        high = logit_grad.astype(bf16)
        low = (logit_grad - high.astype(f32)).astype(bf16)
        both = jnp.concatenate([high, low], axis=0)
        pre_grad = [jnp.concatenate(pre_grads[k : k + 2], axis=1) for k in range(0, kn, 2)]
        wait()
        per = w_ref.shape[0] // n_mp
        width = out_ref.shape[2]
        contract = (((1,), (1,)), ((), ()))
        for m in range(n_mp):
            gw = gw_ref[m * width : (m + 1) * width, :]
            gated = lax.dot_general(both, gw, contract, preferred_element_type=f32)
            acc = gated[:rows] + gated[rows:]
            for k in range(0, kn, 2):
                w = pair_weights(w_ref, k, m * per, (m + 1) * per)
                acc = acc + lax.dot_general(
                    pre_grad[k // 2], w, contract, preferred_element_type=f32
                )
            out_ref[m] = acc.astype(bf16)

    return kernel


def per_device(inputs, expert_w, gate_w, tower_up, tower_out, sections, tasks, labels):
    f32, bf16 = jnp.float32, jnp.bfloat16
    rows, din = inputs.shape
    tn = tasks.shape[1]
    n_mp = lax.axis_size("mp")
    n_sec = NX * NY * NC
    kn = gate_w.shape[2]
    part_d, width = expert_w.shape[1:]
    cols = width // n_mp
    pair_slots = 2 * rows // n_sec
    slots = n_sec * pair_slots
    sec_axes = ("x", "y", "c")

    block = expert_w[0].reshape(part_d, n_mp, cols).transpose(1, 0, 2)
    block = jnp.broadcast_to(block[None], (NY, n_mp, part_d, cols))
    part = lax.all_to_all(
        block.reshape(NY * n_mp, part_d, cols), ("y", "mp"), 0, 0, tiled=True
    )
    wide = lax.all_to_all(
        jnp.broadcast_to(part[None], (NX,) + part.shape), "x", 0, 0, tiled=True
    )
    other = lax.ppermute(wide, "c", [(0, 1), (1, 0)])
    core = jnp.where(lax.axis_index("c") == 0, 0, 1).astype(jnp.int32).reshape(1)
    wide = wide.reshape(NX * NY, kn, part_d, cols)
    other = other.reshape(NX * NY, kn, part_d, cols)
    flat_gate = gate_w.reshape(din, tn * kn)

    gates, row_at, col_at = pl.pallas_call(
        gate_kernel(tn, kn, pair_slots),
        out_shape=(
            jax.ShapeDtypeStruct((rows, tn * kn), f32),
            jax.ShapeDtypeStruct((2 * tn, rows), f32),
            jax.ShapeDtypeStruct((rows, 2 * tn), f32),
        ),
        name="gates",
    )(inputs, flat_gate, sections.reshape(1, n_sec), tasks)

    vmem = pl.BlockSpec(memory_space=pltpu.VMEM)
    smem = pl.BlockSpec(memory_space=pltpu.SMEM)
    anym = pl.BlockSpec(memory_space=pl.ANY)
    w_scratch = [
        pltpu.VMEM((NX * NY, NC, kn, part_d, cols), bf16),
        pltpu.SemaphoreType.DMA((2,)),
    ]
    sent, pre = pl.pallas_call(
        forward_kernel(tn, kn, pair_slots, n_mp),
        out_shape=(
            jax.ShapeDtypeStruct((n_mp, slots, cols), bf16),
            jax.ShapeDtypeStruct((rows, kn * cols), f32),
        ),
        in_specs=[smem, anym, anym, vmem, vmem, vmem],
        out_specs=(vmem, vmem),
        scratch_shapes=w_scratch,
        name="experts",
    )(core, wide, other, inputs, gates, row_at)
    sent = sent.reshape(n_mp * n_sec, pair_slots, cols)
    arrived = lax.all_to_all(sent, ("mp",) + sec_axes, 0, 0, tiled=True)

    up = tower_up[0]
    out_w = tower_out[0].astype(f32)
    rows_in = arrived.reshape(n_mp, slots, cols).transpose(1, 0, 2).reshape(slots, width)
    act = jnp.dot(rows_in, up, preferred_element_type=f32)
    sig_act = jax.nn.sigmoid(act)
    logit_part = jnp.sum(act * sig_act * out_w[None, :], axis=1)
    act_grad = (out_w[None, :] * silu_slope(act, sig_act)).astype(bf16)
    back = lax.dot_general(
        act_grad, up, (((1,), (1,)), ((), ())), preferred_element_type=f32
    ).astype(bf16)
    back = back.reshape(slots, n_mp, cols).transpose(1, 0, 2)
    high, low = split_two(logit_part)
    extra = jnp.concatenate([high.reshape(-1, cols), low.reshape(-1, cols)], axis=0)
    n_extra = extra.shape[0]
    extra = jnp.concatenate([extra, jnp.zeros((16 - n_extra, cols), bf16)], axis=0)
    extra = jnp.broadcast_to(extra[None], (n_mp, 16, cols))
    summed = lax.all_to_all(jnp.concatenate([back, extra], axis=1), "mp", 0, 0, tiled=True)
    total = jnp.sum(summed.astype(f32), axis=0)
    logit = (total[slots : slots + n_extra // 2] + total[slots + n_extra // 2 : slots + n_extra])
    high, low = split_two(logit.reshape(n_sec, pair_slots))
    tail = jnp.concatenate([high, low], axis=1)
    tail = jnp.pad(tail, ((0, 0), (0, cols - 2 * pair_slots)))[:, None]
    body = total[:slots].astype(bf16).reshape(n_sec, pair_slots, cols)
    fill = jnp.zeros((n_sec, 8 - pair_slots - 1, cols), bf16)
    home = lax.all_to_all(
        jnp.concatenate([body, tail, fill], axis=1), sec_axes, 0, 0, tiled=True
    )
    partial = pl.pallas_call(
        backward_kernel(tn, kn, pair_slots, n_mp),
        out_shape=jax.ShapeDtypeStruct((n_mp, rows, din // n_mp), bf16),
        in_specs=[smem, anym, anym] + [vmem] * 7,
        out_specs=vmem,
        scratch_shapes=w_scratch,
        name="grads",
    )(
        core,
        wide,
        other,
        home.reshape(n_sec * 8, cols),
        gates,
        col_at,
        pre,
        labels,
        tasks,
        flat_gate,
    )
    pieces = lax.all_to_all(partial, "mp", 0, 0, tiled=True)
    return jnp.sum(pieces.astype(f32), axis=0).astype(bf16)


def solution(mesh):
    grid = Mesh(
        mesh.devices.reshape(NX, NY, NC, mesh.shape["mp"]), ("x", "y", "c", "mp")
    )
    sec = ("x", "y", "c")
    in_specs = (
        P(sec, None),
        P("mp", sec, None),
        P(),
        P(sec, None, "mp"),
        P(sec, "mp"),
        P(),
        P(sec, None),
        P(sec, None),
    )
    return jax.shard_map(
        per_device, mesh=grid, in_specs=in_specs, out_specs=P(sec, "mp"), check_vma=False
    )
```

time: 205 us -> 184 us (0.90)
  local copies, waits for them, and re-layouts: 29.1 us -> 5.27 us
  Pallas kernels: 0 us -> 16.8 us
  matrix products: 11.5 us -> 1.14 us
  other arithmetic: 6.9 us -> 2.51 us
    pallas_call x0 -> x3, Pallas kernels: none -> 16.8 us  [the longest x1 9.04 us: per_device(): pl.pallas_call(backward_kernel(tn, kn, pair_slots, n_mp), out_shape=jax.S...]
    mul x41 -> x0, local copies, waits for them, and re-layouts: 15.4 us -> none  [the longest x28 13.8 us: per_device(): mixture = mixture + gates[:, :, k, None] * wide_out[:, None, k]]
    dot_general x5 -> x0, matrix products: 9.02 us -> none  [the longest x1 3.74 us: per_device(): lax.dot_general(pre_grad, w_all, (((1,), (1,)), ((), ())), preferred_elem...]
    transpose x1 -> x0, local copies, waits for them, and re-layouts: 4.18 us -> none  [per_device(): w_all = whole.transpose(0, 2, 1, 3).reshape(din, kn * cols)]
    slice x14 -> x0, local copies, waits for them, and re-layouts: 2.35 us -> none  [the longest x1 1.02 us: per_device(): logit_home = rows_back[:, :, cols] + rows_back[:, :, cols + 1]]
  transfers between devices with their start and end apart: 4 -> 4, of which waited for: 3 -> 3; matrix products, arithmetic and copies ran while one was open for 3% -> 1% of each run, Pallas kernels for 0% -> 1%
where the time goes in v2:
time: 184 us; the launch traced here: 183 us
  blocking collectives  81.2 us (44%)
  waiting for transfers between devices  50.9 us (28%)
  starting transfers between devices  25.2 us (14%)
  Pallas kernels  16.8 us (9%)
  local copies, waits for them, and re-layouts  5.27 us (3%)
  other arithmetic  2.51 us (1%)
    all_to_all x1, blocking collectives, per_device(): lax.all_to_all(block.reshape(NY * n_mp, part_d, cols), ('y', 'mp'), 0, 0,...  33.4 us
    all_to_all x1, blocking collectives, per_device(): lax.all_to_all(jnp.broadcast_to(part[None], (NX,) + part.shape), 'x', 0,...  26.5 us
    all_to_all x1, waiting for transfers between devices, per_device(): arrived = lax.all_to_all(sent, ('mp',) + sec_axes, 0, 0, tiled=True)  22.6 us
    all_to_all x1, blocking collectives, per_device(): pieces = lax.all_to_all(partial, 'mp', 0, 0, tiled=True)  21.3 us
    all_to_all x1, waiting for transfers between devices, per_device(): lax.all_to_all(jnp.concatenate([back, extra], axis=1), 'mp', 0, 0, tiled=...  18.6 us
    all_to_all x1, starting transfers between devices, per_device(): arrived = lax.all_to_all(sent, ('mp',) + sec_axes, 0, 0, tiled=True)  10.4 us
    all_to_all x1, waiting for transfers between devices, per_device(): lax.all_to_all(jnp.concatenate([body, tail, fill], axis=1), sec_axes, 0,...  9.7 us
    pallas_call x1, Pallas kernels, per_device(): pl.pallas_call(backward_kernel(tn, kn, pair_slots, n_mp), out_shape=jax.S...  9.04 us
  transfers between devices with their start and end apart: 4, of which 3 were waited for; matrix products, arithmetic and copies ran while one was open for 1% of the time, Pallas kernels for 1%

profile of v2, /device:TPU:1, one launch (start us, length us, event | category | flops | bytes accessed | tf_op | source)
XLA Modules:
  0.0 183.3 jit_solution(251548140538565658)
XLA Ops:
  0.0 0.9 copy.65
  1.0 0.1 broadcast_in_dim.12
  1.1 33.4 %all_to_all.30 = bf16[64,32,128]{2,1,0:T(8,128)(2,1)S(1)} all-to-all(bf16[64,32,128]{2,1,0:T(8,128)(2,1)S(1)} %bitcast.44), channel_id=1, replica_groups=mesh['x'=4,'y'=8,'c'=2,'mp'=8] {'y','mp'}, dimensions={0} | all-to-all | bytes 1048576 | tf_op jit(solution)/shard_map/all_to_all | solution.py:231
  34.4 0.3 broadcast_in_dim.13
  34.8 26.5 %all_to_all.31 = bf16[4,64,32,128]{3,2,1,0:T(8,128)(2,1)S(1)} all-to-all(bf16[4,64,32,128]{3,2,1,0:T(8,128)(2,1)S(1)} %broadcast_in_dim.13), channel_id=1, replica_groups=mesh['x'=4,'y'=8,'c'=2,'mp'=8] {'x'}, dimensions={0} | all-to-all | bytes 4194304 | tf_op jit(solution)/shard_map/all_to_all | solution.py:234
  61.3 6.6 %collective-permute-start = (bf16[4,64,32,128]{3,2,1,0:T(8,128)(2,1)S(1)}, bf16[4,64,32,128]{3,2,1,0:T(8,128)(2,1)}, u32[]{:S(2)}, u32[]{:S(2)}) collective-permute-start(bf16[4,64,32,128]{3,2,1,0:T(8,128)(2,1)S(1)} %all_to_all.31), channel_id=1, source_target_pairs={{0,8},{8,0},{1,9},{9,1},{2,10},{10,2},{3,11},{11,3},{4,12},{12,4},... | collective-permute-start | bytes 6291464 | tf_op jit(solution)/shard_map/ppermute | solution.py:237
  67.9 1.0 copy.51.gw_ref
  69.0 0.7 copy.52.task_ref
  69.7 2.4 %gates.1 = (f32[128,48]{1,0:T(8,128)}, f32[12,128]{1,0:T(8,128)}, f32[128,12]{1,0:T(8,128)}) custom-call(bf16[128,2048]{1,0:T(8,128)(2,1)} %x_ref.3, bf16[2048,48]{1,0:T(8,128)(2,1)} %copy.51.gw_ref, s32[1,64]{1,0:T(1,128)} %bitcast.54, s32[128,6]{1,0:T(8,128)} %copy.52.task_ref), custom_call_target="tpu_custom_call" | custom-call | tf_op jit(solution)/shard_map/gates/pallas_call | solution.py:243
  72.1 5.4 %experts.1 = (bf16[8,256,128]{2,1,0:T(8,128)(2,1)}, f32[128,1024]{1,0:T(8,128)}) custom-call(s32[1]{0:T(128)} %bitcast.core_ref, bf16[32,8,32,128]{3,2,1,0:T(8,128)(2,1)} %bitcast.40, bf16[32,8,32,128]{3,2,1,0:T(8,128)(2,1)} %bitcast.4.other_ref, bf16[128,2048]{1,0:T(8,128)(2,1)} %x_ref.3, f32[128,48]{1,0:T(8,128)} %get-tuple-element.10.gate_ref, ...), custom_call_target="tpu_custom_call" | custom-call | tf_op jit(solution)/shard_map/experts/pallas_call | solution.py:260
  77.5 10.4 %all-to-all-start.2 = ((bf16[512,4,128]{2,1,0:T(4,128)(2,1)}), bf16[512,4,128]{2,1,0:T(4,128)(2,1)S(1)}, u32[]{:S(2)}, u32[]{:S(2)}) async-start(bf16[512,4,128]{2,1,0:T(4,128)(2,1)} %bitcast.46), calls=%async_computation.2 | async-start | bytes 1048576 | tf_op jit(solution)/shard_map/all_to_all | solution.py:272
  87.9 0.1 pad.14.clone
  88.0 22.6 %all-to-all-done.2 = bf16[512,4,128]{2,1,0:T(4,128)(2,1)S(1)} async-done(((bf16[512,4,128]{2,1,0:T(4,128)(2,1)}), bf16[512,4,128]{2,1,0:T(4,128)(2,1)S(1)}, u32[]{:S(2)}, u32[]{:S(2)}) %all-to-all-start.2) | async-done | bytes 524320 | tf_op jit(solution)/shard_map/all_to_all | solution.py:272
  110.6 0.2 copy.53
  110.8 0.6 multiply_reduce_fusion
  111.5 0.5 fusion
  112.0 0.1 copy.67
  112.1 0.1 maximum_maximum_fusion.1
  112.2 0.9 pad_maximum_fusion
  113.1 3.7 %all-to-all-start.3 = ((bf16[8,272,128]{2,1,0:T(8,128)(2,1)}), bf16[8,272,128]{2,1,0:T(8,128)(2,1)S(1)}, u32[]{:S(2)}, u32[]{:S(2)}) async-start(bf16[8,272,128]{2,1,0:T(8,128)(2,1)} %pad_maximum_fusion), calls=%async_computation.3 | async-start | bytes 1114112 | tf_op jit(solution)/shard_map/all_to_all | solution.py:290
  116.8 0.1 pad.7.clone
  116.8 18.6 %all-to-all-done.3 = bf16[8,272,128]{2,1,0:T(8,128)(2,1)S(1)} async-done(((bf16[8,272,128]{2,1,0:T(8,128)(2,1)}), bf16[8,272,128]{2,1,0:T(8,128)(2,1)S(1)}, u32[]{:S(2)}, u32[]{:S(2)}) %all-to-all-start.3) | async-done | bytes 557088 | tf_op jit(solution)/shard_map/all_to_all | solution.py:290
  135.5 0.1 reshape.57
  135.7 0.1 copy.58
  135.8 0.7 maximum_maximum_fusion
  136.6 4.5 %all-to-all-start.4 = ((bf16[64,8,128]{2,1,0:T(8,128)(2,1)}), bf16[64,8,128]{2,1,0:T(8,128)(2,1)S(1)}, u32[]{:S(2)}, u32[]{:S(2)}) async-start(bf16[64,8,128]{2,1,0:T(8,128)(2,1)} %maximum_maximum_fusion), calls=%async_computation.4 | async-start | bytes 262144 | tf_op jit(solution)/shard_map/all_to_all | solution.py:298
  141.1 0.7 copy.59.label_ref
  141.8 9.7 %all-to-all-done.4 = bf16[64,8,128]{2,1,0:T(8,128)(2,1)S(1)} async-done(((bf16[64,8,128]{2,1,0:T(8,128)(2,1)}), bf16[64,8,128]{2,1,0:T(8,128)(2,1)S(1)}, u32[]{:S(2)}, u32[]{:S(2)}) %all-to-all-start.4) | async-done | bytes 131104 | tf_op jit(solution)/shard_map/all_to_all | solution.py:298
  151.5 0.6 copy-done.2
  152.2 9.0 %grads.1 = bf16[8,128,256]{2,1,0:T(8,128)(2,1)} custom-call(s32[1]{0:T(128)} %bitcast.core_ref, bf16[32,8,32,128]{3,2,1,0:T(8,128)(2,1)} %bitcast.41, bf16[32,8,32,128]{3,2,1,0:T(8,128)(2,1)} %bitcast.4.other_ref, bf16[512,128]{1,0:T(8,128)(2,1)} %bitcast.45, f32[128,48]{1,0:T(8,128)} %get-tuple-element.10.gate_ref, f32[128,12]{1,0:T(8,128)} %get-tuple-element.13.col_ref, ...), custom_call_target="tpu_custom_call" | custom-call | tf_op jit(solution)/shard_map/grads/pallas_call | solution.py:301
  161.2 21.3 %all_to_all.32 = bf16[8,128,256]{2,1,0:T(8,128)(2,1)S(1)} all-to-all(bf16[8,128,256]{2,1,0:T(8,128)(2,1)} %grads.1), channel_id=1, replica_groups=mesh['x'=4,'y'=8,'c'=2,'mp'=8] {'mp'}, dimensions={0} | all-to-all | bytes 1048576 | tf_op jit(solution)/shard_map/all_to_all | solution.py:320
  182.6 0.7 reduce_sum.35
  (26 shorter events, 0.3 us)
Async XLA Ops:
  0.0 110.8 %copy-start = (bf16[1,1024,512]{2,1,0:T(8,128)(2,1)S(1)}, bf16[1,1024,512]{2,1,0:T(8,128)(2,1)}, u32[]{:S(2)}) copy-start(bf16[1,1024,512]{2,1,0:T(8,128)(2,1)} %param.11) | copy-start | bytes 3145732
  34.8 33.2 %copy-start.3 = (bf16[2048,6,8]{0,2,1:T(8,128)(2,1)S(1)}, bf16[2048,6,8]{0,2,1:T(8,128)(2,1)}, u32[]{:S(2)}) copy-start(bf16[2048,6,8]{0,2,1:T(8,128)(2,1)} %param.10) | copy-start | bytes 589828
  34.8 34.2 %copy-start.4 = (s32[128,6]{0,1:T(8,128)S(1)}, s32[128,6]{0,1:T(8,128)}, u32[]{:S(2)}) copy-start(s32[128,6]{0,1:T(8,128)} %param.14) | copy-start | bytes 9220
  61.3 10.8 %copy-start.1 = (bf16[4,64,32,128]{3,2,1,0:T(8,128)(2,1)}, bf16[4,64,32,128]{3,2,1,0:T(8,128)(2,1)S(1)}, u32[]{:S(2)}) copy-start(bf16[4,64,32,128]{3,2,1,0:T(8,128)(2,1)S(1)} %all_to_all.31) | copy-start | bytes 6291460
  61.3 10.8 %collective-permute-start = (bf16[4,64,32,128]{3,2,1,0:T(8,128)(2,1)S(1)}, bf16[4,64,32,128]{3,2,1,0:T(8,128)(2,1)}, u32[]{:S(2)}, u32[]{:S(2)}) collective-permute-start(bf16[4,64,32,128]{3,2,1,0:T(8,128)(2,1)S(1)} %all_to_all.31), channel_id=1, source_target_pairs={{0,8},{8,0},{1,9},{9,1},{2,10},{10,2},{3,11},{11,3},{4,12},{12,4},... | collective-permute-start | bytes 6291464 | tf_op jit(solution)/shard_map/ppermute | solution.py:237
  72.1 15.8 %copy-start.6 = (bf16[1,512]{1,0:T(2,128)(2,1)S(1)}, bf16[1,512]{1,0:T(2,128)(2,1)}, u32[]{:S(2)}) copy-start(bf16[1,512]{1,0:T(2,128)(2,1)} %param.12) | copy-start | bytes 3076
  77.5 33.1 %all-to-all-start.2 = ((bf16[512,4,128]{2,1,0:T(4,128)(2,1)}), bf16[512,4,128]{2,1,0:T(4,128)(2,1)S(1)}, u32[]{:S(2)}, u32[]{:S(2)}) async-start(bf16[512,4,128]{2,1,0:T(4,128)(2,1)} %bitcast.46), calls=%async_computation.2 | async-start | bytes 1048576 | tf_op jit(solution)/shard_map/all_to_all | solution.py:272
  113.1 28.0 %copy-start.5 = (s32[128,6]{0,1:T(8,128)S(1)}, s32[128,6]{0,1:T(8,128)}, u32[]{:S(2)}) copy-start(s32[128,6]{0,1:T(8,128)} %param.15) | copy-start | bytes 9220
  113.1 22.3 %all-to-all-start.3 = ((bf16[8,272,128]{2,1,0:T(8,128)(2,1)}), bf16[8,272,128]{2,1,0:T(8,128)(2,1)S(1)}, u32[]{:S(2)}, u32[]{:S(2)}) async-start(bf16[8,272,128]{2,1,0:T(8,128)(2,1)} %pad_maximum_fusion), calls=%async_computation.3 | async-start | bytes 1114112 | tf_op jit(solution)/shard_map/all_to_all | solution.py:290
  136.6 15.0 %all-to-all-start.4 = ((bf16[64,8,128]{2,1,0:T(8,128)(2,1)}), bf16[64,8,128]{2,1,0:T(8,128)(2,1)S(1)}, u32[]{:S(2)}, u32[]{:S(2)}) async-start(bf16[64,8,128]{2,1,0:T(8,128)(2,1)} %maximum_maximum_fusion), calls=%async_computation.4 | async-start | bytes 262144 | tf_op jit(solution)/shard_map/all_to_all | solution.py:298
  151.5 0.7 copy-start.2

commit v3 on v2

v3 whole, which is shorter than its diff:
```python
import jax
import jax.numpy as jnp
from jax import lax
from jax.experimental import pallas as pl
from jax.experimental.pallas import tpu as pltpu
from jax.sharding import Mesh, PartitionSpec as P

loss_scale = 64.0
NX, NY, NC = 4, 8, 2


def silu_slope(value, sig):
    return sig * (1.0 + value * (1.0 - sig))


def split_two(value):
    high = lax.reduce_precision(value, 8, 7)
    return high.astype(jnp.bfloat16), (value - high).astype(jnp.bfloat16)


def gate_kernel(tn, kn, pair_slots):
    f32, bf16 = jnp.float32, jnp.bfloat16

    def kernel(x_ref, gw_ref, sec_ref, task_ref, gate_ref, row_ref):
        logit = lax.dot_general(
            gw_ref[...], x_ref[...], (((1,), (1,)), ((), ())), preferred_element_type=f32
        )
        raised = jnp.exp(logit)
        for t in range(tn):
            part = raised[t * kn : (t + 1) * kn]
            gate_ref[t * kn : (t + 1) * kn, :] = part / jnp.sum(part, axis=0, keepdims=True)

        n_sec = sec_ref.shape[1]
        rows = task_ref.shape[1]
        sec_row = sec_ref[...]
        task = task_ref[...].astype(f32)
        one = lax.broadcasted_iota(jnp.int32, (rows, rows), 0)
        two = lax.broadcasted_iota(jnp.int32, (rows, rows), 1)
        above = (one < two).astype(f32).astype(bf16)
        rank = jnp.dot(task.astype(bf16), above, preferred_element_type=f32)
        ids = lax.broadcasted_iota(jnp.int32, (tn, n_sec), 0)
        member = jnp.sum((sec_row == ids).astype(f32), axis=1, keepdims=True)
        first = jnp.sum((sec_row < ids).astype(f32), axis=1, keepdims=True)
        turn = jnp.zeros_like(rank)
        for step in range(1, pair_slots):
            turn = turn + (rank >= step * member).astype(f32)
        target = first + rank - turn * member
        row_ref[0:tn, :] = jnp.where(task > 0.5, target, -1000.0)
        row_ref[tn : 2 * tn, :] = turn

    return kernel


def load_weights(core_ref, own_ref, other_ref, w_ref, sems):
    def run(own_at, finish):
        first = pltpu.make_async_copy(own_ref, w_ref.at[:, own_at], sems.at[0])
        second = pltpu.make_async_copy(other_ref, w_ref.at[:, 1 - own_at], sems.at[1])
        if finish:
            first.wait()
            second.wait()
        else:
            first.start()
            second.start()

    def both(finish):
        @pl.when(core_ref[0] == 0)
        def _():
            run(0, finish)

        @pl.when(core_ref[0] != 0)
        def _():
            run(1, finish)

    return lambda: both(False), lambda: both(True)


def pair_weights(w_ref, k, lo, hi):
    part_d, cols = w_ref.shape[3:]
    count = (hi - lo) * w_ref.shape[1] * part_d
    return jnp.concatenate(
        [w_ref[lo:hi, :, k + i].reshape(count, cols) for i in range(2)], axis=1
    )


def place_picks(row_ref, tn, total, stride, offsets):
    f32 = jnp.float32
    rows = row_ref.shape[1]
    slot_id = lax.broadcasted_iota(jnp.int32, (total, rows), 0).astype(f32)
    picks = []
    for t in range(tn):
        place = row_ref[t : t + 1, :] * stride + offsets(t)
        picks.append((slot_id == place).astype(f32).astype(jnp.bfloat16))
    return jnp.concatenate(picks, axis=1)


def forward_kernel(tn, kn, pair_slots, n_mp):
    f32, bf16 = jnp.float32, jnp.bfloat16

    def kernel(core_ref, own_ref, other_ref, x_ref, gate_ref, row_ref, sent_ref, pre_ref, w_ref, sems):
        start, wait = load_weights(core_ref, own_ref, other_ref, w_ref, sems)
        start()
        rows = x_ref.shape[0]
        slots, cols = sent_ref.shape[1:]
        pick = place_picks(
            row_ref, tn, slots, pair_slots, lambda t: row_ref[tn + t : tn + t + 1, :]
        )
        wait()
        x = x_ref[...]
        mix = [jnp.zeros((cols, rows), f32) for _ in range(tn)]
        for k in range(0, kn, 2):
            both = jnp.dot(
                x, pair_weights(w_ref, k, 0, w_ref.shape[0]), preferred_element_type=f32
            )
            for i in range(2):
                pre = both[:, i * cols : (i + 1) * cols].T
                pre_ref[k + i] = pre
                out = (pre * jax.nn.sigmoid(pre)).astype(bf16).astype(f32)
                for t in range(tn):
                    at = t * kn + k + i
                    mix[t] = mix[t] + gate_ref[at : at + 1, :] * out
        stack = jnp.concatenate([m.astype(bf16) for m in mix], axis=1)
        sent = lax.dot_general(
            pick, stack, (((1,), (1,)), ((), ())), preferred_element_type=f32
        ).astype(bf16)
        for m in range(n_mp):
            sent_ref[m] = sent

    return kernel


def backward_kernel(tn, kn, pair_slots, n_mp):
    f32, bf16 = jnp.float32, jnp.bfloat16

    def kernel(
        core_ref, own_ref, other_ref, home_ref, gate_ref, row_ref, pre_ref,
        label_ref, task_ref, gw_ref, out_ref, w_ref, sems,
    ):
        start, wait = load_weights(core_ref, own_ref, other_ref, w_ref, sems)
        start()
        total, cols = home_ref.shape
        rows = gate_ref.shape[1]
        home = home_ref[...]
        pick = place_picks(
            row_ref, tn, total, 8.0, lambda t: row_ref[tn + t : tn + t + 1, :]
        )
        pick_tail = place_picks(row_ref, tn, total, 8.0, lambda t: float(pair_slots))
        down = (((0,), (0,)), ((), ()))
        got = lax.dot_general(home, pick, down, preferred_element_type=f32)
        tail = lax.dot_general(home, pick_tail, down, preferred_element_type=f32)
        sub = lax.broadcasted_iota(jnp.int32, (8, rows), 0)
        grads = []
        for t in range(tn):
            turn = row_ref[tn + t : tn + t + 1, :].astype(jnp.int32)
            chosen = (sub == turn) | (sub == turn + pair_slots)
            part = tail[0:8, t * rows : (t + 1) * rows]
            logit = jnp.sum(jnp.where(chosen, part, 0.0), axis=0, keepdims=True)
            label = label_ref[t : t + 1, :].astype(f32)
            alive = task_ref[t : t + 1, :].astype(f32)
            slope = loss_scale * (jax.nn.sigmoid(logit) - label) * alive
            grads.append(
                (slope * got[:, t * rows : (t + 1) * rows]).astype(bf16).astype(f32)
            )
        sub_k = lax.broadcasted_iota(jnp.int32, (kn, rows), 0)
        gate_grads = [jnp.zeros((kn, rows), f32) for _ in range(tn)]
        pre_grads = []
        for k in range(kn):
            pre = pre_ref[k]
            sig = jax.nn.sigmoid(pre)
            out = (pre * sig).astype(bf16).astype(f32)
            grad = jnp.zeros((cols, rows), f32)
            for t in range(tn):
                at = t * kn + k
                grad = grad + gate_ref[at : at + 1, :] * grads[t]
                dot = jnp.sum(grads[t] * out, axis=0, keepdims=True)
                gate_grads[t] = jnp.where(sub_k == k, dot, gate_grads[t])
            pre_grads.append((grad * silu_slope(pre, sig)).T.astype(bf16))
        highs, lows = [], []
        for t in range(tn):
            gate = gate_ref[t * kn : (t + 1) * kn, :]
            spread = jnp.sum(gate * gate_grads[t], axis=0, keepdims=True)
            logit_grad = gate * (gate_grads[t] - spread)
            high = logit_grad.astype(bf16).astype(f32)
            highs.append(high)
            lows.append(logit_grad - high)
        blank = rows - 2 * tn * kn
        fill = [jnp.zeros((blank, rows), f32)]
        both = jnp.concatenate(highs + lows + fill, axis=0).T.astype(bf16)
        pre_grad = [jnp.concatenate(pre_grads[k : k + 2], axis=1) for k in range(0, kn, 2)]
        wait()
        per = w_ref.shape[0] // n_mp
        width = out_ref.shape[2]
        contract = (((1,), (1,)), ((), ()))
        for m in range(n_mp):
            gw = gw_ref[:, m * width : (m + 1) * width]
            gw = jnp.concatenate([gw, gw, jnp.zeros((blank, width), bf16)], axis=0)
            acc = jnp.dot(both, gw, preferred_element_type=f32)
            for k in range(0, kn, 2):
                w = pair_weights(w_ref, k, m * per, (m + 1) * per)
                acc = acc + lax.dot_general(
                    pre_grad[k // 2], w, contract, preferred_element_type=f32
                )
            out_ref[m] = acc.astype(bf16)

    return kernel


def per_device(inputs, expert_w, gate_w, tower_up, tower_out, sections, tasks, labels):
    f32, bf16 = jnp.float32, jnp.bfloat16
    rows, din = inputs.shape
    tn = tasks.shape[1]
    n_mp = lax.axis_size("mp")
    n_sec = NX * NY * NC
    kn = gate_w.shape[2]
    part_d, width = expert_w.shape[1:]
    cols = width // n_mp
    pair_slots = 2 * rows // n_sec
    slots = n_sec * pair_slots
    sec_axes = ("x", "y", "c")

    block = expert_w[0].reshape(part_d, n_mp, cols).transpose(1, 0, 2)
    block = jnp.broadcast_to(block[None], (NY, n_mp, part_d, cols))
    part = lax.all_to_all(
        block.reshape(NY * n_mp, part_d, cols), ("y", "mp"), 0, 0, tiled=True
    )
    wide = lax.all_to_all(
        jnp.broadcast_to(part[None], (NX,) + part.shape), "x", 0, 0, tiled=True
    )
    other = lax.ppermute(wide, "c", [(0, 1), (1, 0)])
    core = jnp.where(lax.axis_index("c") == 0, 0, 1).astype(jnp.int32).reshape(1)
    wide = wide.reshape(NX * NY, kn, part_d, cols)
    other = other.reshape(NX * NY, kn, part_d, cols)
    flat_gate = gate_w.transpose(1, 2, 0).reshape(tn * kn, din)
    task_rows = tasks.T

    gates, row_at = pl.pallas_call(
        gate_kernel(tn, kn, pair_slots),
        out_shape=(
            jax.ShapeDtypeStruct((tn * kn, rows), f32),
            jax.ShapeDtypeStruct((2 * tn, rows), f32),
        ),
        name="gates",
    )(inputs, flat_gate, sections.reshape(1, n_sec), task_rows)

    vmem = pl.BlockSpec(memory_space=pltpu.VMEM)
    smem = pl.BlockSpec(memory_space=pltpu.SMEM)
    anym = pl.BlockSpec(memory_space=pl.ANY)
    w_scratch = [
        pltpu.VMEM((NX * NY, NC, kn, part_d, cols), bf16),
        pltpu.SemaphoreType.DMA((2,)),
    ]
    sent, pre = pl.pallas_call(
        forward_kernel(tn, kn, pair_slots, n_mp),
        out_shape=(
            jax.ShapeDtypeStruct((n_mp, slots, cols), bf16),
            jax.ShapeDtypeStruct((kn, cols, rows), f32),
        ),
        in_specs=[smem, anym, anym, vmem, vmem, vmem],
        out_specs=(vmem, vmem),
        scratch_shapes=w_scratch,
        name="experts",
    )(core, wide, other, inputs, gates, row_at)
    sent = sent.reshape(n_mp * n_sec, pair_slots, cols)
    arrived = lax.all_to_all(sent, ("mp",) + sec_axes, 0, 0, tiled=True)

    up = tower_up[0]
    out_w = tower_out[0].astype(f32)
    rows_in = arrived.reshape(n_mp, slots, cols).transpose(1, 0, 2).reshape(slots, width)
    act = jnp.dot(rows_in, up, preferred_element_type=f32)
    sig_act = jax.nn.sigmoid(act)
    logit_part = jnp.sum(act * sig_act * out_w[None, :], axis=1)
    act_grad = (out_w[None, :] * silu_slope(act, sig_act)).astype(bf16)
    back = lax.dot_general(
        act_grad, up, (((1,), (1,)), ((), ())), preferred_element_type=f32
    ).astype(bf16)
    back = back.reshape(slots, n_mp, cols).transpose(1, 0, 2)
    high, low = split_two(logit_part)
    extra = jnp.concatenate([high.reshape(-1, cols), low.reshape(-1, cols)], axis=0)
    n_extra = extra.shape[0]
    extra = jnp.concatenate([extra, jnp.zeros((16 - n_extra, cols), bf16)], axis=0)
    extra = jnp.broadcast_to(extra[None], (n_mp, 16, cols))
    summed = lax.all_to_all(jnp.concatenate([back, extra], axis=1), "mp", 0, 0, tiled=True)
    total = jnp.sum(summed.astype(f32), axis=0)
    logit = (total[slots : slots + n_extra // 2] + total[slots + n_extra // 2 : slots + n_extra])
    high, low = split_two(logit.reshape(n_sec, pair_slots))
    tail = jnp.concatenate([high, low], axis=1)
    tail = jnp.pad(tail, ((0, 0), (0, cols - 2 * pair_slots)))[:, None]
    body = total[:slots].astype(bf16).reshape(n_sec, pair_slots, cols)
    fill = jnp.zeros((n_sec, 8 - pair_slots - 1, cols), bf16)
    home = lax.all_to_all(
        jnp.concatenate([body, tail, fill], axis=1), sec_axes, 0, 0, tiled=True
    )
    partial = pl.pallas_call(
        backward_kernel(tn, kn, pair_slots, n_mp),
        out_shape=jax.ShapeDtypeStruct((n_mp, rows, din // n_mp), bf16),
        in_specs=[smem, anym, anym] + [vmem] * 7,
        out_specs=vmem,
        scratch_shapes=w_scratch,
        name="grads",
    )(
        core,
        wide,
        other,
        home.reshape(n_sec * 8, cols),
        gates,
        row_at,
        pre,
        labels.T,
        task_rows,
        flat_gate,
    )
    pieces = lax.all_to_all(partial, "mp", 0, 0, tiled=True)
    return jnp.sum(pieces.astype(f32), axis=0).astype(bf16)


def solution(mesh):
    grid = Mesh(
        mesh.devices.reshape(NX, NY, NC, mesh.shape["mp"]), ("x", "y", "c", "mp")
    )
    sec = ("x", "y", "c")
    in_specs = (
        P(sec, None),
        P("mp", sec, None),
        P(),
        P(sec, None, "mp"),
        P(sec, "mp"),
        P(),
        P(sec, None),
        P(sec, None),
    )
    return jax.shard_map(
        per_device, mesh=grid, in_specs=in_specs, out_specs=P(sec, "mp"), check_vma=False
    )
```

time: 184 us -> 179 us (0.973)
  blocking collectives: 81.2 us -> 95.9 us
  waiting for transfers between devices: 50.9 us -> 43 us
  starting transfers between devices: 25.2 us -> 20.8 us
  Pallas kernels: 16.8 us -> 13.2 us
  local copies, waits for them, and re-layouts: 5.27 us -> 2.11 us
    all_to_all x0 -> x1, blocking collectives: none -> 14.8 us  [per_device(): lax.all_to_all(jnp.concatenate([body, tail, fill], axis=1), sec_axes, 0,...]
    all_to_all x1 -> x0, waiting for transfers between devices: 9.7 us -> none  [per_device(): lax.all_to_all(jnp.concatenate([body, tail, fill], axis=1), sec_axes, 0,...]
    all_to_all x1 -> x0, starting transfers between devices: 4.52 us -> none  [per_device(): lax.all_to_all(jnp.concatenate([body, tail, fill], axis=1), sec_axes, 0,...]
    pallas_call x1, Pallas kernels: 9.04 us -> 5.86 us  [per_device(): pl.pallas_call(backward_kernel(tn, kn, pair_slots, n_mp), out_shape=jax.S...]
    unnamed x17 -> x7, local copies, waits for them, and re-layouts: 3.09 us -> 0.95 us
  transfers between devices with their start and end apart: 4 -> 3, of which waited for: 3 -> 3; matrix products, arithmetic and copies ran while one was open for 1% -> 0% of each run, Pallas kernels for 1% -> 1%
where the time goes in v3:
time: 179 us; the launch traced here: 178 us
  blocking collectives  95.9 us (54%)
  waiting for transfers between devices  43 us (24%)
  starting transfers between devices  20.8 us (12%)
  Pallas kernels  13.2 us (7%)
  local copies, waits for them, and re-layouts  2.11 us (1%)
  other arithmetic  1.83 us (1%)
    all_to_all x1, blocking collectives, per_device(): lax.all_to_all(block.reshape(NY * n_mp, part_d, cols), ('y', 'mp'), 0, 0,...  33.4 us
    all_to_all x1, blocking collectives, per_device(): lax.all_to_all(jnp.broadcast_to(part[None], (NX,) + part.shape), 'x', 0,...  26.4 us
    all_to_all x1, waiting for transfers between devices, per_device(): arrived = lax.all_to_all(sent, ('mp',) + sec_axes, 0, 0, tiled=True)  22.6 us
    all_to_all x1, blocking collectives, per_device(): pieces = lax.all_to_all(partial, 'mp', 0, 0, tiled=True)  21.3 us
    all_to_all x1, waiting for transfers between devices, per_device(): lax.all_to_all(jnp.concatenate([back, extra], axis=1), 'mp', 0, 0, tiled=...  18.6 us
    all_to_all x1, blocking collectives, per_device(): lax.all_to_all(jnp.concatenate([body, tail, fill], axis=1), sec_axes, 0,...  14.8 us
    all_to_all x1, starting transfers between devices, per_device(): arrived = lax.all_to_all(sent, ('mp',) + sec_axes, 0, 0, tiled=True)  10.6 us
    ppermute x1, starting transfers between devices, per_device(): other = lax.ppermute(wide, 'c', [(0, 1), (1, 0)])  6.63 us
  transfers between devices with their start and end apart: 3, of which 3 were waited for; matrix products, arithmetic and copies ran while one was open for 0% of the time, Pallas kernels for 1%

profile of v3, /device:TPU:1, one launch (start us, length us, event | category | flops | bytes accessed | tf_op | source)
XLA Modules:
  0.0 178.1 jit_solution(16797983713159919169)
XLA Ops:
  0.0 0.9 copy.36
  1.0 0.1 broadcast_in_dim.12
  1.1 33.4 %all_to_all.30 = bf16[64,32,128]{2,1,0:T(8,128)(2,1)S(1)} all-to-all(bf16[64,32,128]{2,1,0:T(8,128)(2,1)S(1)} %bitcast.48), channel_id=1, replica_groups=mesh['x'=4,'y'=8,'c'=2,'mp'=8] {'y','mp'}, dimensions={0} | all-to-all | bytes 1048576 | tf_op jit(solution)/shard_map/all_to_all | solution.py:222
  34.4 0.3 broadcast_in_dim.13
  34.8 26.4 %all_to_all.31 = bf16[4,64,32,128]{3,2,1,0:T(8,128)(2,1)S(1)} all-to-all(bf16[4,64,32,128]{3,2,1,0:T(8,128)(2,1)S(1)} %broadcast_in_dim.13), channel_id=1, replica_groups=mesh['x'=4,'y'=8,'c'=2,'mp'=8] {'x'}, dimensions={0} | all-to-all | bytes 4194304 | tf_op jit(solution)/shard_map/all_to_all | solution.py:225
  61.1 6.6 %collective-permute-start = (bf16[4,64,32,128]{3,2,1,0:T(8,128)(2,1)S(1)}, bf16[4,64,32,128]{3,2,1,0:T(8,128)(2,1)}, u32[]{:S(2)}, u32[]{:S(2)}) collective-permute-start(bf16[4,64,32,128]{3,2,1,0:T(8,128)(2,1)S(1)} %all_to_all.31), channel_id=1, source_target_pairs={{0,8},{8,0},{1,9},{9,1},{2,10},{10,2},{3,11},{11,3},{4,12},{12,4},... | collective-permute-start | bytes 6291464 | tf_op jit(solution)/shard_map/ppermute | solution.py:228
  67.8 2.1 %gates.1 = (f32[48,128]{1,0:T(8,128)}, f32[12,128]{1,0:T(8,128)}) custom-call(bf16[128,2048]{1,0:T(8,128)(2,1)} %x_ref.3, bf16[48,2048]{1,0:T(8,128)(2,1)} %bitcast.49, s32[1,64]{1,0:T(1,128)} %bitcast.62, s32[6,128]{1,0:T(8,128)} %bitcast.57), custom_call_target="tpu_custom_call" | custom-call | tf_op jit(solution)/shard_map/gates/pallas_call | solution.py:235
  69.9 1.8 %collective-permute-done = bf16[4,64,32,128]{3,2,1,0:T(8,128)(2,1)} collective-permute-done((bf16[4,64,32,128]{3,2,1,0:T(8,128)(2,1)S(1)}, bf16[4,64,32,128]{3,2,1,0:T(8,128)(2,1)}, u32[]{:S(2)}, u32[]{:S(2)}) %collective-permute-start) | collective-permute-done | bytes 2097184 | tf_op jit(solution)/shard_map/ppermute | solution.py:228
  71.7 0.0 copy-done.1
  71.7 5.3 %experts.1 = (bf16[8,256,128]{2,1,0:T(8,128)(2,1)}, f32[8,128,128]{2,1,0:T(8,128)}) custom-call(s32[1]{0:T(128)} %bitcast.core_ref, bf16[32,8,32,128]{3,2,1,0:T(8,128)(2,1)} %bitcast.44, bf16[32,8,32,128]{3,2,1,0:T(8,128)(2,1)} %bitcast.4.other_ref, bf16[128,2048]{1,0:T(8,128)(2,1)} %x_ref.3, f32[48,128]{1,0:T(8,128)} %get-tuple-element.9.gate_ref, ...), custom_call_target="tpu_custom_call" | custom-call | tf_op jit(solution)/shard_map/experts/pallas_call | solution.py:251
  76.9 10.6 %all-to-all-start.2 = ((bf16[512,4,128]{2,1,0:T(4,128)(2,1)}), bf16[512,4,128]{2,1,0:T(4,128)(2,1)S(1)}, u32[]{:S(2)}, u32[]{:S(2)}) async-start(bf16[512,4,128]{2,1,0:T(4,128)(2,1)} %bitcast.52), calls=%async_computation.2 | async-start | bytes 1048576 | tf_op jit(solution)/shard_map/all_to_all | solution.py:263
  87.6 0.0 copy-done.2
  87.6 0.1 pad.14.clone
  87.7 22.6 %all-to-all-done.2 = bf16[512,4,128]{2,1,0:T(4,128)(2,1)S(1)} async-done(((bf16[512,4,128]{2,1,0:T(4,128)(2,1)}), bf16[512,4,128]{2,1,0:T(4,128)(2,1)S(1)}, u32[]{:S(2)}, u32[]{:S(2)}) %all-to-all-start.2) | async-done | bytes 524320 | tf_op jit(solution)/shard_map/all_to_all | solution.py:263
  110.3 0.2 copy.27
  110.5 0.6 multiply_reduce_fusion
  111.1 0.5 fusion
  111.7 0.1 copy.38
  111.8 0.1 maximum_maximum_fusion.1
  111.9 0.8 pad_maximum_fusion
  112.7 3.5 %all-to-all-start.3 = ((bf16[8,272,128]{2,1,0:T(8,128)(2,1)}), bf16[8,272,128]{2,1,0:T(8,128)(2,1)S(1)}, u32[]{:S(2)}, u32[]{:S(2)}) async-start(bf16[8,272,128]{2,1,0:T(8,128)(2,1)} %pad_maximum_fusion), calls=%async_computation.3 | async-start | bytes 1114112 | tf_op jit(solution)/shard_map/all_to_all | solution.py:281
  116.2 0.1 pad.7.clone
  116.3 18.6 %all-to-all-done.3 = bf16[8,272,128]{2,1,0:T(8,128)(2,1)S(1)} async-done(((bf16[8,272,128]{2,1,0:T(8,128)(2,1)}), bf16[8,272,128]{2,1,0:T(8,128)(2,1)S(1)}, u32[]{:S(2)}, u32[]{:S(2)}) %all-to-all-start.3) | async-done | bytes 557088 | tf_op jit(solution)/shard_map/all_to_all | solution.py:281
  134.9 0.1 convert_reduce_fusion
  135.0 0.1 reshape.57
  135.1 0.1 copy.29
  135.2 0.1 copy.32
  135.3 0.1 maximum_maximum_fusion
  135.4 14.8 %all_to_all.32 = bf16[64,8,128]{2,1,0:T(8,128)(2,1)} all-to-all(bf16[64,8,128]{2,1,0:T(8,128)(2,1)S(1)} %maximum_maximum_fusion), channel_id=1, replica_groups=mesh['x'=4,'y'=8,'c'=2,'mp'=8] {'x','y','c'}, dimensions={0} | all-to-all | bytes 262144 | tf_op jit(solution)/shard_map/all_to_all | solution.py:289
  150.2 5.9 %grads.1 = bf16[8,128,256]{2,1,0:T(8,128)(2,1)} custom-call(s32[1]{0:T(128)} %bitcast.core_ref, bf16[32,8,32,128]{3,2,1,0:T(8,128)(2,1)} %bitcast.45, bf16[32,8,32,128]{3,2,1,0:T(8,128)(2,1)} %bitcast.4.other_ref, bf16[512,128]{1,0:T(8,128)(2,1)} %bitcast.51, f32[48,128]{1,0:T(8,128)} %get-tuple-element.9.gate_ref, f32[12,128]{1,0:T(8,128)} %get-tuple-element.10.row_ref, ...), custom_call_target="tpu_custom_call" | custom-call | tf_op jit(solution)/shard_map/grads/pallas_call | solution.py:292
  156.1 21.3 %all_to_all.33 = bf16[8,128,256]{2,1,0:T(8,128)(2,1)S(1)} all-to-all(bf16[8,128,256]{2,1,0:T(8,128)(2,1)} %grads.1), channel_id=1, replica_groups=mesh['x'=4,'y'=8,'c'=2,'mp'=8] {'mp'}, dimensions={0} | all-to-all | bytes 1048576 | tf_op jit(solution)/shard_map/all_to_all | solution.py:311
  177.4 0.7 reduce_sum.35
  (14 shorter events, 0.1 us)
Async XLA Ops:
  0.0 110.5 %copy-start = (bf16[1,1024,512]{2,1,0:T(8,128)(2,1)S(1)}, bf16[1,1024,512]{2,1,0:T(8,128)(2,1)}, u32[]{:S(2)}) copy-start(bf16[1,1024,512]{2,1,0:T(8,128)(2,1)} %param.11) | copy-start | bytes 3145732
  61.1 10.5 %copy-start.1 = (bf16[4,64,32,128]{3,2,1,0:T(8,128)(2,1)}, bf16[4,64,32,128]{3,2,1,0:T(8,128)(2,1)S(1)}, u32[]{:S(2)}) copy-start(bf16[4,64,32,128]{3,2,1,0:T(8,128)(2,1)S(1)} %all_to_all.31) | copy-start | bytes 6291460
  61.1 10.5 %collective-permute-start = (bf16[4,64,32,128]{3,2,1,0:T(8,128)(2,1)S(1)}, bf16[4,64,32,128]{3,2,1,0:T(8,128)(2,1)}, u32[]{:S(2)}, u32[]{:S(2)}) collective-permute-start(bf16[4,64,32,128]{3,2,1,0:T(8,128)(2,1)S(1)} %all_to_all.31), channel_id=1, source_target_pairs={{0,8},{8,0},{1,9},{9,1},{2,10},{10,2},{3,11},{11,3},{4,12},{12,4},... | collective-permute-start | bytes 6291464 | tf_op jit(solution)/shard_map/ppermute | solution.py:228
  71.7 15.9 %copy-start.2 = (bf16[1,512]{1,0:T(2,128)(2,1)S(1)}, bf16[1,512]{1,0:T(2,128)(2,1)}, u32[]{:S(2)}) copy-start(bf16[1,512]{1,0:T(2,128)(2,1)} %param.12) | copy-start | bytes 3076
  76.9 33.3 %all-to-all-start.2 = ((bf16[512,4,128]{2,1,0:T(4,128)(2,1)}), bf16[512,4,128]{2,1,0:T(4,128)(2,1)S(1)}, u32[]{:S(2)}, u32[]{:S(2)}) async-start(bf16[512,4,128]{2,1,0:T(4,128)(2,1)} %bitcast.52), calls=%async_computation.2 | async-start | bytes 1048576 | tf_op jit(solution)/shard_map/all_to_all | solution.py:263
  112.7 22.2 %all-to-all-start.3 = ((bf16[8,272,128]{2,1,0:T(8,128)(2,1)}), bf16[8,272,128]{2,1,0:T(8,128)(2,1)S(1)}, u32[]{:S(2)}, u32[]{:S(2)}) async-start(bf16[8,272,128]{2,1,0:T(8,128)(2,1)} %pad_maximum_fusion), calls=%async_computation.3 | async-start | bytes 1114112 | tf_op jit(solution)/shard_map/all_to_all | solution.py:281
